TPU v7x, 32 devices: a whole 2x2x4 slice. The times are simulated.
32 devices in a mesh: pix: 16 (over z, y, x), lat: 2 (over core).
Axes of the slice: x: 2, y: 2, z: 4, core: 2. Of those that a mesh axis runs over, the one named last changes fastest.
Arguments:
- latents: bfloat16 [8192, 512], P('pix'), may hold values from -6 to 6
- w_send: bfloat16 [512, 512], P(None, 'lat'), may hold values from -0.25 to 0.25
- w_recv: bfloat16 [512, 512], P(None, 'lat'), may hold values from -0.25 to 0.25
- edge_bias: float32 [512], P('lat'), may hold values from -3 to 3
- w_msg: bfloat16 [512, 512], P('lat'), may hold values from -0.25 to 0.25
- w_self: bfloat16 [512, 512], P(None, 'lat'), may hold values from -0.25 to 0.25
- w_agg: bfloat16 [512, 512], P(None, 'lat'), may hold values from -0.25 to 0.25
- node_bias: float32 [512], P('lat'), may hold values from -3 to 3
- w_node: bfloat16 [512, 512], P('lat'), may hold values from -0.25 to 0.25
- norm_gain: float32 [512], replicated, may hold values from 0.25 to 1.75
- coarse_ids: int32 [128], P('pix'), may hold values from 0 to 511
- send_list: int32 [16], P('pix'), may hold values from 0 to 3
- recv_tile: int32 [512], P('pix'), may hold values from 0 to 3
- send_tile: int32 [512], P('pix'), may hold values from 0 to 6, as said below
- edge_ends: int32 [512, 2, 128], P('pix'), may hold values from 0 to 127
- edge_mask: int32 [512, 128], P('pix'), may hold values 0 or 1
- cotangent: bfloat16 [8192, 512], P('pix'), may hold values from -6 to 6
Outputs:
- new_latents: bfloat16 [8192, 512], P('pix')
- grad_latents: float32 [8192, 512], P('pix', 'lat')
- grad_w_send: float32 [512, 512], P(None, 'lat')
- grad_w_recv: float32 [512, 512], P(None, 'lat')
- grad_edge_bias: float32 [512], P('lat')
- grad_w_msg: float32 [512, 512], P('lat')
- grad_w_self: float32 [512, 512], P(None, 'lat')
- grad_w_agg: float32 [512, 512], P(None, 'lat')
- grad_node_bias: float32 [512], P('lat')
- grad_w_node: float32 [512, 512], P('lat')
- grad_gain: float32 [512], replicated
Inputs may be any that keep to these rules, and one draw needn't show every extreme that they name: `send_tile`: a block's sender tile, numbered as in the first step: first the device's own tiles, then the 1 lent tiles of the preceding and of the following pixel range, then the 1 tiles of the coarse panel; in each device's own run of 32 blocks, the first names a tile lent by the preceding range and the second one lent by the following range. `coarse_ids`: rows may repeat.
All inputs are finite; a program needn't handle non-finite values. No bound on the sum of `edge_mask` on one device may be relied on, other than what follows from the above.
Results may differ from a plain program's by a relative error of at most 0.0085.
Values may be sent and summed in bfloat16 or wider, within the bound.
A program may use at most 128 MiB of HBM per device.

v0:
```python
import math

import jax
import jax.numpy as jnp
from jax import lax
from jax.sharding import PartitionSpec as P

norm_eps = 1e-05


def from_behind(block, axis, distance):
    devices = range(lax.axis_size(axis))
    route = [((i - distance) % len(devices), i) for i in devices]
    return lax.ppermute(block, axis, route)


def silu_slope(values):
    sigma = jax.nn.sigmoid(values)
    return sigma * (1.0 + values * (1.0 - sigma))


def tile_sums(values, offsets, weights, block_tiles, tile_count):
    block_count, tile_len = offsets.shape
    width = values.shape[-1]
    positions = jnp.arange(tile_len, dtype=jnp.int32)
    incidence = (offsets[:, :, None] == positions[None, None, :]).astype(jnp.float32) * weights[
        :, :, None
    ]
    per_block = jnp.einsum(
        "ben,beh->bnh",
        incidence,
        values.reshape(block_count, tile_len, width),
        precision=lax.Precision.HIGHEST,
    )
    tile_ids = jnp.arange(tile_count, dtype=jnp.int32)
    selector = (block_tiles[None, :] == tile_ids[:, None]).astype(jnp.float32)
    summed = jnp.einsum("tb,bnh->tnh", selector, per_block, precision=lax.Precision.HIGHEST)
    return summed.reshape(tile_count * tile_len, width)


def shards(
    latents,
    w_send,
    w_recv,
    edge_bias,
    w_msg,
    w_self,
    w_agg,
    node_bias,
    w_node,
    norm_gain,
    coarse_ids,
    send_list,
    recv_tile,
    send_tile,
    edge_ends,
    edge_mask,
    cotangent,
):
    node_dev, latent_width = latents.shape
    tile_len = edge_ends.shape[2]
    tiles_dev = node_dev // tile_len
    halo_rows = send_list.shape[0] * tile_len
    pix_count = lax.axis_size("pix")
    lat_count = lax.axis_size("lat")
    grad_scale = 1.0 / math.sqrt(node_dev * pix_count)
    hidden_part = w_send.shape[1]
    send_proj = jnp.dot(latents, w_send, preferred_element_type=jnp.float32)
    recv_proj = jnp.dot(latents, w_recv, preferred_element_type=jnp.float32)
    lent_rows = latents.reshape(tiles_dev, tile_len, latent_width)[send_list].reshape(
        halo_rows, latent_width
    )
    from_left = from_behind(lent_rows, "pix", 1)
    from_right = from_behind(lent_rows, "pix", -1)
    side_proj = jnp.dot(
        jnp.concatenate([from_left, from_right], axis=0), w_send, preferred_element_type=jnp.float32
    )
    panel_proj = jnp.dot(
        lax.all_gather(latents[coarse_ids], "pix", axis=0, tiled=True),
        w_send,
        preferred_element_type=jnp.float32,
    )
    source_proj = jnp.concatenate([send_proj, side_proj, panel_proj], axis=0)
    source_tiles = source_proj.shape[0] // tile_len
    sender_offs = edge_ends[:, 0, :]
    receiver_offs = edge_ends[:, 1, :]
    senders = (send_tile[:, None] * tile_len + sender_offs).reshape(-1)
    receivers = (recv_tile[:, None] * tile_len + receiver_offs).reshape(-1)
    mask_rows = edge_mask.astype(jnp.float32)
    edge_weight = mask_rows.reshape(-1)
    unit_rows = jnp.ones_like(mask_rows)
    edge_pre = source_proj[senders] + recv_proj[receivers] + edge_bias
    edge_act = jax.nn.silu(edge_pre).astype(jnp.bfloat16)
    message = jnp.dot(edge_act, w_msg, preferred_element_type=jnp.float32)
    agg_part = tile_sums(message, receiver_offs, mask_rows, recv_tile, tiles_dev)
    aggregate = lax.psum(agg_part, "lat")
    aggregate_bf = aggregate.astype(jnp.bfloat16)
    node_pre = (
        jnp.dot(latents, w_self, preferred_element_type=jnp.float32)
        + jnp.dot(aggregate_bf, w_agg, preferred_element_type=jnp.float32)
        + node_bias
    )
    node_act = jax.nn.silu(node_pre).astype(jnp.bfloat16)
    out_part = jnp.dot(node_act, w_node, preferred_element_type=jnp.float32)
    node_out = lax.psum(out_part, "lat")
    row_mean = jnp.mean(node_out, axis=-1, keepdims=True)
    centered = node_out - row_mean
    row_var = jnp.mean(centered * centered, axis=-1, keepdims=True)
    inv_std = lax.rsqrt(row_var + norm_eps)
    normed = centered * inv_std
    new_latents = (latents.astype(jnp.float32) + normed * norm_gain).astype(jnp.bfloat16)
    grad_out = cotangent.astype(jnp.float32)
    gain_sum = jnp.sum(grad_out * normed, axis=0)
    d_normed = grad_out * norm_gain
    out_cot = inv_std * (
        d_normed
        - jnp.mean(d_normed, axis=-1, keepdims=True)
        - normed * jnp.mean(d_normed * normed, axis=-1, keepdims=True)
    )
    out_cot_bf = out_cot.astype(jnp.bfloat16)
    node_w_grad = jnp.dot(node_act.T, out_cot_bf, preferred_element_type=jnp.float32)
    node_pre_cot = jnp.dot(out_cot_bf, w_node.T, preferred_element_type=jnp.float32) * silu_slope(
        node_pre
    )
    node_bias_sum = jnp.sum(node_pre_cot, axis=0)
    node_pre_bf = node_pre_cot.astype(jnp.bfloat16)
    self_w_grad = jnp.dot(latents.T, node_pre_bf, preferred_element_type=jnp.float32)
    agg_w_grad = jnp.dot(aggregate_bf.T, node_pre_bf, preferred_element_type=jnp.float32)
    latent_part = jnp.dot(node_pre_bf, w_self.T, preferred_element_type=jnp.float32)
    agg_cot_part = jnp.dot(node_pre_bf, w_agg.T, preferred_element_type=jnp.float32)
    agg_cot = lax.psum(agg_cot_part, "lat")
    agg_cot_bf = agg_cot.astype(jnp.bfloat16)
    msg_cot = agg_cot_bf[receivers] * edge_weight.astype(jnp.bfloat16)[:, None]
    msg_w_grad = jnp.dot(edge_act.T, msg_cot, preferred_element_type=jnp.float32)
    pre_cot = jnp.dot(msg_cot, w_msg.T, preferred_element_type=jnp.float32) * silu_slope(edge_pre)
    edge_bias_sum = jnp.sum(pre_cot, axis=0)
    src_cot = tile_sums(pre_cot, sender_offs, unit_rows, send_tile, source_tiles)
    dst_cot = tile_sums(pre_cot, receiver_offs, unit_rows, recv_tile, tiles_dev)
    own_grad = src_cot[:node_dev]
    left_back = src_cot[node_dev : node_dev + halo_rows]
    right_back = src_cot[node_dev + halo_rows : node_dev + 2 * halo_rows]
    panel_part = src_cot[node_dev + 2 * halo_rows :]
    to_left_owner = from_behind(left_back.astype(jnp.bfloat16), "pix", -1).astype(left_back.dtype)
    to_right_owner = from_behind(right_back.astype(jnp.bfloat16), "pix", 1).astype(right_back.dtype)
    returned = (to_left_owner + to_right_owner).reshape(send_list.shape[0], tile_len, hidden_part)
    own_grad = own_grad.reshape(tiles_dev, tile_len, hidden_part).at[send_list].add(returned)
    own_grad = own_grad.reshape(node_dev, hidden_part)
    coarse_grad = lax.psum_scatter(panel_part, "pix", scatter_dimension=0, tiled=True)
    own_grad = own_grad.at[coarse_ids].add(coarse_grad)
    src_cot_bf = own_grad.astype(jnp.bfloat16)
    dst_cot_bf = dst_cot.astype(jnp.bfloat16)
    send_w_grad = jnp.dot(latents.T, src_cot_bf, preferred_element_type=jnp.float32)
    recv_w_grad = jnp.dot(latents.T, dst_cot_bf, preferred_element_type=jnp.float32)
    latent_part = (
        latent_part
        + jnp.dot(src_cot_bf, w_send.T, preferred_element_type=jnp.float32)
        + jnp.dot(dst_cot_bf, w_recv.T, preferred_element_type=jnp.float32)
    )
    share_width = latent_width // lat_count
    lat_index = lax.axis_index("lat")
    lat_share = lax.psum_scatter(
        latent_part.astype(jnp.bfloat16), "lat", scatter_dimension=1, tiled=True
    ).astype(jnp.float32)
    grad_latents = lat_share + lax.dynamic_slice_in_dim(
        grad_out, lat_index * share_width, share_width, 1
    )
    summed = lax.psum(
        (
            send_w_grad,
            recv_w_grad,
            edge_bias_sum,
            msg_w_grad,
            self_w_grad,
            agg_w_grad,
            node_bias_sum,
            node_w_grad,
            gain_sum,
        ),
        "pix",
    )
    scaled = [grad_scale * entry for entry in summed]
    return (
        new_latents,
        grad_latents,
        scaled[0],
        scaled[1],
        scaled[2],
        scaled[3],
        scaled[4],
        scaled[5],
        scaled[6],
        scaled[7],
        scaled[8],
    )


def solution(mesh):
    return jax.shard_map(
        shards,
        mesh=mesh,
        in_specs=(
            P("pix", None),
            P(None, "lat"),
            P(None, "lat"),
            P("lat"),
            P("lat", None),
            P(None, "lat"),
            P(None, "lat"),
            P("lat"),
            P("lat", None),
            P(),
            P("pix"),
            P("pix"),
            P("pix"),
            P("pix"),
            P("pix", None, None),
            P("pix", None),
            P("pix", None),
        ),
        out_specs=(
            P("pix", None),
            P("pix", "lat"),
            P(None, "lat"),
            P(None, "lat"),
            P("lat"),
            P("lat", None),
            P(None, "lat"),
            P(None, "lat"),
            P("lat"),
            P("lat", None),
            P(),
        ),
        check_vma=False,
    )
```

profile of v0, /device:TPU:0, one launch (start us, length us, event | category | flops | bytes accessed | tf_op | source)
XLA Modules:
  0.0 465.3 jit_solution(5024926762899600851)
XLA Ops:
  8.9 3.0 collective-permute-start
  11.9 4.1 collective-permute-start.1
  16.6 1.7 gather_fusion
  18.3 38.1 %all-gather = bf16[128,512]{1,0:T(8,128)(2,1)S(1)} all-gather(bf16[8,512]{1,0:T(8,128)(2,1)S(1)} %gather_fusion), channel_id=2, replica_groups=mesh['pix'=16,'lat'=2] {'pix'}, dimensions={0}, use_global_device_ids=true | all-gather | bytes 139264 | tf_op jit(solution)/shard_map/all_gather | solution.py:79
  56.4 1.4 fusion.52
  57.8 1.1 fusion.53
  62.2 1.4 fusion.54
  63.6 1.2 fusion.51
  64.9 16.1 %gather_fusion.2 = f32[4096,256]{1,0:T(8,128)} fusion(f32[512,256]{1,0:T(8,128)S(1)} %fusion.54, s32[4096]{0:T(1024)S(1)} %broadcast_clamp_fusion), kind=kCustom, calls=%fused_computation.2 | custom fusion | bytes 8404992 | tf_op jit(solution)/shard_map/gather | solution.py:92
  81.3 16.2 %gather_fusion.1 = f32[4096,256]{1,0:T(8,128)} fusion(f32[896,256]{1,0:T(8,128)S(1)} %pad_maximum_fusion, s32[4096]{0:T(1024)S(1)} %broadcast_clamp_fusion.1), kind=kCustom, calls=%fused_computation.1 | custom fusion | bytes 8404992 | tf_op jit(solution)/shard_map/gather | solution.py:92
  97.6 4.9 %multiply_convert_fusion = bf16[4096,256]{1,0:T(8,128)(2,1)S(1)} fusion(f32[256]{0:T(256)S(1)} %copy-done.22, f32[4096,256]{1,0:T(8,128)} %gather_fusion.1, f32[4096,256]{1,0:T(8,128)} %gather_fusion.2), kind=kLoop, calls=%fused_computation.12 | loop fusion | flops 7340032 | bytes 10486784 | tf_op jit(solution)/shard_map/convert_element_type | solution.py:93
  102.5 1.3 fusion.55
  103.8 8.5 %fusion.11 = f32[32,128,512]{2,1,0:T(8,128)S(1)} fusion(f32[32,128,512]{2,1,0:T(8,128)S(1)} %bitcast.85, f32[32,128]{1,0:T(8,128)S(1)} %get-tuple-element.101, s32[32,128]{1,0:T(8,128)S(1)} %bitcast.94), kind=kOutput, calls=%fused_computation.21 | convolution fusion | flops 3222274048 | bytes 16809984 | tf_op jit(solution)/shard_map/ben,beh->bnh/dot_general | solution.py:29
  112.4 7.7 %fusion = f32[4,128,512]{2,0,1:T(4,128)S(1)} fusion(f32[32,128,512]{2,1,0:T(8,128)S(1)} %fusion.11, s32[32]{0:T(128)S(1)} %copy-done.20), kind=kOutput, calls=%fused_computation.5 | convolution fusion | flops 100663424 | bytes 9437312 | tf_op jit(solution)/shard_map/tb,bnh->tnh/dot_general | solution.py:37
  120.5 6.3 %all-reduce.10 = bf16[512,512]{1,0:T(8,128)(2,1)S(1)} all-reduce(f32[512,512]{1,0:T(8,128)S(1)} %bitcast.90), channel_id=1, replica_groups=mesh['pix'=16,'lat'=2] {'lat'}, use_global_device_ids=true, to_apply=%region_0.1 | all-reduce | flops 262144 | bytes 1572864 | tf_op jit(solution)/shard_map/psum | solution.py:96
  126.8 1.3 fusion.16
  128.9 2.2 fusion.45
  131.9 15.1 %all-reduce.7.cloned.1.call-done = f32[512,512]{1,0:T(8,128)} async-done(((f32[512,512]{1,0:T(8,128)}), f32[512,512]{1,0:T(8,128)}) %all-reduce.7.cloned.1.call-update) | async-done | bytes 1048592 | tf_op jit(solution)/shard_map/psum | solution.py:105
  147.0 1.5 reduce_sum.63
  148.5 1.5 multiply_reduce_fusion.2
  150.1 1.8 multiply_reduce_fusion
  151.9 1.3 multiply_convert_fusion.1
  153.5 1.2 fusion.44
  155.0 1.1 fusion.58
  156.2 1.3 fusion.56
  157.5 6.3 %all-reduce.11 = bf16[512,512]{1,0:T(8,128)(2,1)S(1)} all-reduce(f32[512,512]{1,0:T(8,128)S(1)} %fusion.57), channel_id=1, replica_groups=mesh['pix'=16,'lat'=2] {'lat'}, use_global_device_ids=true, to_apply=%region_6.7 | all-reduce | flops 262144 | bytes 1572864 | tf_op jit(solution)/shard_map/psum | solution.py:131
  163.8 17.7 %gather_fusion.3 = bf16[4096,512]{1,0:T(8,128)(2,1)} fusion(bf16[512,512]{1,0:T(8,128)(2,1)S(1)} %all-reduce.11, s32[4096]{0:T(1024)S(1)} %broadcast_clamp_fusion), kind=kCustom, calls=%fused_computation.3 | custom fusion | bytes 8404992 | tf_op jit(solution)/shard_map/gather | solution.py:133
  181.5 5.9 %fusion.50 = (f32[256]{0:T(256)S(1)}, f32[4096,256]{1,0:T(8,128)S(1)}) fusion(f32[256]{0:T(256)S(1)} %copy-done.22, f32[4096,256]{1,0:T(8,128)} %gather_fusion.1, f32[4096,256]{1,0:T(8,128)} %gather_fusion.2, bf16[256,512]{1,0:T(8,128)(2,1)S(1)} %copy-done, bf16[4096,512]{1,0:T(8,128)(2,1)} %gather_fusion.3, bf16[4096]{0:T(1024)(128)(2,1)S(1)} %get-tuple-element.100), kind=kOutput, calls=%fused_computation.107 | convolution fusion | flops 1087373056 | bytes 17049600 | tf_op jit(solution)/shard_map/dot_general | solution.py:135
  187.4 4.4 fusion.13
  191.8 2.7 fusion.14
  194.5 3.8 fusion.49
  198.6 5.5 %collective-permute-start.2 = (bf16[128,256]{1,0:T(8,128)(2,1)S(1)}, bf16[128,256]{1,0:T(8,128)(2,1)S(1)}, u32[]{:S(2)}, u32[]{:S(2)}) collective-permute-start(bf16[128,256]{1,0:T(8,128)(2,1)S(1)} %bitcast.97), channel_id=1, source_target_pairs={{2,0},{4,2},{6,4},{8,6},{10,8},{12,10},{14,12},{16,14},{18,16},{20... | collective-permute-start | bytes 196616 | tf_op jit(solution)/shard_map/ppermute | solution.py:14
  205.3 5.8 %fusion.17 = bf16[4,128,256]{2,0,1:T(4,128)(2,1)S(1)} fusion(f32[32,128,256]{2,1,0:T(8,128)} %fusion.13, s32[32]{0:T(128)S(1)} %copy-done.20), kind=kOutput, calls=%fused_computation.35 | convolution fusion | flops 50462848 | bytes 4456576 | tf_op jit(solution)/shard_map/tb,bnh->tnh/dot_general | solution.py:37
  211.8 1.1 convolution_bitcast_fusion.1
  213.8 1.9 broadcast_select_fusion
  215.7 4.1 scatter-add.12
  219.8 1.1 copy.56
  220.9 61.5 %reduce-scatter.3.cloned.1.call-done = f32[8,256]{1,0:T(8,128)} async-done(((f32[128,256]{1,0:T(8,128)}), f32[8,256]{1,0:T(8,128)}) %reduce-scatter.3.cloned.1.call-update) | async-done | bytes 8208 | tf_op jit(solution)/shard_map/reduce_scatter | solution.py:148
  283.5 1.6 convolution_add_fusion.1
  285.1 2.2 fusion.15
  287.3 2.1 convolution_bitcast_fusion
  289.4 4.5 fusion.6
  293.9 1.1 convolution_bitcast_fusion.2
  295.2 38.7 %all-reduce = (f32[256]{0:T(256)S(1)}, f32[256]{0:T(256)S(1)}, f32[512]{0:T(512)S(1)}) all-reduce(f32[256]{0:T(256)S(1)} %get-tuple-element.105, f32[256]{0:T(256)S(1)} %get-tuple-element.92, f32[512]{0:T(512)S(1)} %get-tuple-element.78), channel_id=1, replica_groups=mesh['pix'=16,'lat'=2] {'pix'}, use_global_device_ids=true, to_apply=%region_14.15 | all-reduce | flops 1024 | bytes 8192 | tf_op jit(solution)/shard_map/psum | solution.py:167
  335.6 1.8 dynamic-slice_add_fusion
  337.4 113.0 %all-reduce.9.cloned.1.call-done = (f32[512,256]{0,1:T(8,128)}, f32[512,256]{0,1:T(8,128)}, f32[256,512]{1,0:T(8,128)}, f32[512,256]{0,1:T(8,128)}, f32[512,256]{0,1:T(8,128)}, /*index=5*/f32[256,512]{1,0:T(8,128)}) async-done(((f32[512,256]{0,1:T(8,128)}, f32[512,256]{0,1:T(8,128)}, f32[256,512]{1,0:T(8,128)}, f32[512,256]{0,1:T(8,128)}, f32[512,256]{0,1:T(8,128)}, /*index=5*/f32[256,512]{1,0:T(8,128)}), ...) | async-done | bytes 3145744 | tf_op jit(solution)/shard_map/psum | solution.py:167
  450.5 1.2 broadcast_multiply_fusion.5
  452.7 1.1 broadcast_multiply_fusion.4
  (108 shorter events, 19.6 us)
Async XLA Ops:
  7.2 95.3 %copy-start = (bf16[256,512]{1,0:T(8,128)(2,1)S(1)}, bf16[256,512]{1,0:T(8,128)(2,1)}, u32[]{:S(2)}) copy-start(bf16[256,512]{1,0:T(8,128)(2,1)} %param.23) | copy-start | bytes 786436
  7.2 56.4 %copy-start.1 = (bf16[512,512]{1,0:T(8,128)(2,1)S(1)}, bf16[512,512]{1,0:T(8,128)(2,1)}, u32[]{:S(2)}) copy-start(bf16[512,512]{1,0:T(8,128)(2,1)} %param.19) | copy-start | bytes 1572868
  7.2 139.8 %all-reduce.7.cloned.1.call-start = ((), (), s32[]{:S(2)}) async-start(), calls=%async_computation.2 | async-start | bytes 2097152 | tf_op jit(solution)/shard_map/psum | solution.py:105
  8.9 72.1 %collective-permute-start = (bf16[128,512]{1,0:T(8,128)(2,1)S(1)}, bf16[128,512]{1,0:T(8,128)(2,1)S(1)}, u32[]{:S(2)}, u32[]{:S(2)}) collective-permute-start(bf16[128,512]{1,0:T(8,128)(2,1)S(1)} %dynamic-slice_bitcast_fusion), channel_id=1, source_target_pairs={{30,0},{0,2},{2,4},{4,6},{6,8},{8,10},{10,12},{12,14},{14,16},{16,... | collective-permute-start | bytes 393224 | tf_op jit(solution)/shard_map/ppermute | solution.py:14
  11.9 69.1 %collective-permute-start.1 = (bf16[128,512]{1,0:T(8,128)(2,1)S(1)}, bf16[128,512]{1,0:T(8,128)(2,1)S(1)}, u32[]{:S(2)}, u32[]{:S(2)}) collective-permute-start(bf16[128,512]{1,0:T(8,128)(2,1)S(1)} %dynamic-slice_bitcast_fusion), channel_id=1, source_target_pairs={{2,0},{4,2},{6,4},{8,6},{10,8},{12,10},{14,12},{16,14},{18,16},{20... | collective-permute-start | bytes 393224 | tf_op jit(solution)/shard_map/ppermute | solution.py:14
  64.9 16.1 %copy-start.18 = (s32[32,128]{1,0:T(8,128)S(1)}, s32[32,128]{1,0:T(8,128)}, u32[]{:S(2)}) copy-start(s32[32,128]{1,0:T(8,128)} %param.34) | copy-start | bytes 49156
  64.9 16.1 %copy-start.8 = (bf16[512,256]{1,0:T(8,128)(2,1)S(1)}, bf16[512,256]{1,0:T(8,128)(2,1)}, u32[]{:S(2)}) copy-start(bf16[512,256]{1,0:T(8,128)(2,1)} %param.20) | copy-start | bytes 786436
  81.3 16.3 %copy-start.22 = (f32[256]{0:T(256)S(1)}, f32[256]{0:T(256)}, u32[]{:S(2)}) copy-start(f32[256]{0:T(256)} %param.22) | copy-start | bytes 3076
  102.5 1.3 copy-start.3
  103.8 8.5 %copy-start.20 = (s32[32]{0:T(128)S(1)}, s32[32]{0:T(128)}, u32[]{:S(2)}) copy-start(s32[32]{0:T(128)} %param.31) | copy-start | bytes 388
  112.4 14.4 %copy-start.21 = (f32[256]{0:T(256)S(1)}, f32[256]{0:T(256)}, u32[]{:S(2)}) copy-start(f32[256]{0:T(256)} %param.26) | copy-start | bytes 3076
  120.1 11.1 %copy-start.24 = (s32[3]{0:T(128)S(1)}, s32[3]{0:T(128)}, u32[]{:S(2)}) copy-start(s32[3]{0:T(128)} %constant.62.clone.1) | copy-start | bytes 40
  126.8 23.3 %copy-start.5 = (bf16[512,512]{1,0:T(8,128)(2,1)S(1)}, bf16[512,512]{1,0:T(8,128)(2,1)}, u32[]{:S(2)}) copy-start(bf16[512,512]{1,0:T(8,128)(2,1)} %param.35) | copy-start | bytes 1572868
  126.8 23.3 %copy-start.19 = (f32[512]{0:T(512)S(1)}, f32[512]{0:T(512)}, u32[]{:S(2)}) copy-start(f32[512]{0:T(512)} %param.28) | copy-start | bytes 6148
  128.1 0.8 copy-start.12
  131.1 22.0 %copy-start.13 = (f32[512,256]{1,0:T(8,128)S(1)}, f32[512,256]{1,0:T(8,128)}, u32[]{:S(2)}) copy-start(f32[512,256]{1,0:T(8,128)} %copy-done.12) | copy-start | bytes 1572868
  131.1 151.3 %reduce-scatter.3.cloned.1.call-start = ((), (), s32[]{:S(2)}) async-start(), calls=%async_computation.3 | async-start | bytes 139264 | tf_op jit(solution)/shard_map/reduce_scatter | solution.py:148
  147.0 4.8 %copy-start.2 = (f32[512,512]{1,0:T(8,128)S(1)}, f32[512,512]{1,0:T(8,128)}, u32[]{:S(2)}) copy-start(f32[512,512]{1,0:T(8,128)} %all-reduce.7.cloned.1.call-done) | copy-start | bytes 3145732
  148.5 4.7 copy-start.25
  153.1 1.6 copy-start.10
  153.1 3.0 copy-start.11
  153.5 2.7 copy-start.7
  191.8 2.7 copy-start.23
  198.6 15.2 %collective-permute-start.2 = (bf16[128,256]{1,0:T(8,128)(2,1)S(1)}, bf16[128,256]{1,0:T(8,128)(2,1)S(1)}, u32[]{:S(2)}, u32[]{:S(2)}) collective-permute-start(bf16[128,256]{1,0:T(8,128)(2,1)S(1)} %bitcast.97), channel_id=1, source_target_pairs={{2,0},{4,2},{6,4},{8,6},{10,8},{12,10},{14,12},{16,14},{18,16},{20... | collective-permute-start | bytes 196616 | tf_op jit(solution)/shard_map/ppermute | solution.py:14
  204.2 9.7 %collective-permute-start.3 = (bf16[128,256]{1,0:T(8,128)(2,1)S(1)}, bf16[128,256]{1,0:T(8,128)(2,1)S(1)}, u32[]{:S(2)}, u32[]{:S(2)}) collective-permute-start(bf16[128,256]{1,0:T(8,128)(2,1)S(1)} %bitcast.98), channel_id=1, source_target_pairs={{30,0},{0,2},{2,4},{4,6},{6,8},{8,10},{10,12},{12,14},{14,16},{16,... | collective-permute-start | bytes 196616 | tf_op jit(solution)/shard_map/ppermute | solution.py:14
  205.1 130.6 %reduce-scatter.5.cloned.1.call-start = ((), (), s32[]{:S(2)}) async-start(), calls=%async_computation.4 | async-start | bytes 786432 | tf_op jit(solution)/shard_map/reduce_scatter | solution.py:161
  211.1 0.7 copy-start.9
  215.7 73.7 %copy-start.4 = (bf16[4096,256]{1,0:T(8,128)(2,1)S(1)}, bf16[4096,256]{1,0:T(8,128)(2,1)}, u32[]{:S(2)}) copy-start(bf16[4096,256]{1,0:T(8,128)(2,1)} %copy-done.3) | copy-start | bytes 6291460
  287.3 163.2 %all-reduce.9.cloned.1.call-start = ((), (), s32[]{:S(2)}) async-start(), calls=%async_computation.5 | async-start | bytes 6291456 | tf_op jit(solution)/shard_map/psum | solution.py:167
  293.9 1.2 copy-start.6
  450.5 4.3 copy-start.17
  450.5 5.4 %copy-start.16 = (f32[512,256]{0,1:T(8,128)S(1)}, f32[512,256]{0,1:T(8,128)}, u32[]{:S(2)}) copy-start(f32[512,256]{0,1:T(8,128)} %get-tuple-element.88) | copy-start | bytes 1572868
  450.5 6.4 %copy-start.15 = (f32[256,512]{1,0:T(8,128)S(1)}, f32[256,512]{1,0:T(8,128)}, u32[]{:S(2)}) copy-start(f32[256,512]{1,0:T(8,128)} %get-tuple-element.89) | copy-start | bytes 1572868
  451.7 6.1 %copy-start.14 = (f32[256,512]{1,0:T(8,128)S(1)}, f32[256,512]{1,0:T(8,128)}, u32[]{:S(2)}) copy-start(f32[256,512]{1,0:T(8,128)} %get-tuple-element.86) | copy-start | bytes 1572868
Sparse Core Ops, SparseCore 0:
  131.3 15.7 all-reduce.6
  205.2 77.1 reduce-scatter.2
  287.4 4.3 reduce-scatter.4
  299.8 150.6 all-reduce.8
where the time goes:
time: 469 us; the launch traced here: 465 us
  waiting for transfers between devices  190 us (41%)
  blocking collectives  89.4 us (19%)
  local copies, waits for them, and re-layouts  66.8 us (14%)
  matrix products  65.9 us (14%)
  other arithmetic  25.2 us (5%)
  between operations  15.2 us (3%)
  starting transfers between devices  13 us (3%)
    psum x1, waiting for transfers between devices, shards(): lax.psum((send_w_grad, recv_w_grad, edge_bias_sum, msg_w_grad, self_w_gra...  113 us
    reduce_scatter x1, waiting for transfers between devices, shards(): lax.psum_scatter(panel_part, 'pix', scatter_dimension=0, tiled=True)  61.5 us
    psum x1, blocking collectives, shards(): lax.psum((send_w_grad, recv_w_grad, edge_bias_sum, msg_w_grad, self_w_gra...  38.7 us
    all_gather x1, blocking collectives, shards(): lax.all_gather(latents[coarse_ids], 'pix', axis=0, tiled=True)  38.1 us
    gather x2, local copies, waits for them, and re-layouts, shards(): edge_pre = source_proj[senders] + recv_proj[receivers] + edge_bias  32.3 us
    gather x1, local copies, waits for them, and re-layouts, shards(): msg_cot = agg_cot_bf[receivers] * edge_weight.astype(jnp.bfloat16)[:, None]  17.7 us
    dot_general x3, matrix products, tile_sums(): jnp.einsum('tb,bnh->tnh', selector, per_block, precision=lax.Precision.HI...  17.3 us
    dot_general x3, matrix products, tile_sums(): jnp.einsum('ben,beh->bnh', incidence, values.reshape(block_count, tile_le...  15.6 us
  transfers between devices with their start and end apart: 8, of which 3 were waited for; matrix products, arithmetic and copies ran while one was open for 12% of the time, Pallas kernels for 0%

commit v1 on v0

v1 whole, which is shorter than its diff:
```python
import functools
import math

import jax
import jax.numpy as jnp
from jax import lax
from jax.experimental import pallas as pl
from jax.experimental.pallas import tpu as pltpu
from jax.sharding import PartitionSpec as P

norm_eps = 1e-05
f32 = jnp.float32
bf16 = jnp.bfloat16
MESH = pl.DeviceIdType.MESH
VM = pl.BlockSpec(memory_space=pltpu.VMEM)
SM = pl.BlockSpec(memory_space=pltpu.SMEM)
PLANE = 4
GROUPS = 2
LIMIT = 60 * 1024 * 1024


def dot(a, b):
    return jnp.dot(a, b, preferred_element_type=f32)


def dot_tn(a, b):
    return lax.dot_general(a, b, (((0,), (0,)), ((), ())), preferred_element_type=f32)


def dot_nt(a, b):
    return lax.dot_general(a, b, (((1,), (1,)), ((), ())), preferred_element_type=f32)


def sigmoid(v):
    return 0.5 * jnp.tanh(0.5 * v) + 0.5


def remote(src, dst, send, recv, where):
    return pltpu.make_async_remote_copy(
        src_ref=src, dst_ref=dst, send_sem=send, recv_sem=recv, device_id=where, device_id_type=MESH
    )


def enter(pix_count, partner):
    me = lax.axis_index("pix")
    barrier = pltpu.get_barrier_semaphore()
    total = 0
    for d in range(1, pix_count):
        to = lax.rem(me + d, pix_count)
        pl.semaphore_signal(barrier, inc=1, device_id={"pix": to}, device_id_type=MESH)
        total += 1
    if partner:
        other = 1 - lax.axis_index("lat")
        pl.semaphore_signal(barrier, inc=1, device_id={"lat": other}, device_id_type=MESH)
        total += 1
    pl.semaphore_wait(barrier, total)


def comm_call(body, outs, ins, scratch, cid, flops=10**8, byts=10**6):
    return pl.pallas_call(
        body,
        out_shape=outs,
        in_specs=ins,
        out_specs=[VM] * len(outs),
        scratch_shapes=scratch,
        compiler_params=pltpu.CompilerParams(
            collective_id=cid, has_side_effects=True, vmem_limit_bytes=LIMIT
        ),
        cost_estimate=pl.CostEstimate(flops=flops, bytes_accessed=byts, transcendentals=0),
    )


def share_kernel(
    n, lat_ref, lent_ref, coarse_ref, ws_ref, wr_ref, wm_ref, wn_ref, wa_ref,
    src_ref, rcv_ref, wm_out, wn_out, wa_out,
    halo, panel, wm, wn, wa, ssem, rsem, csend, crecv,
):
    me = lax.axis_index("pix")
    lat = lax.axis_index("lat")
    other = 1 - lat
    right = lax.rem(me + 1, n)
    left = lax.rem(me + n - 1, n)
    enter(n, True)
    copies = [
        remote(lent_ref, halo.at[0], ssem.at[0], rsem.at[0], {"pix": right}),
        remote(lent_ref, halo.at[1], ssem.at[1], rsem.at[1], {"pix": left}),
    ]
    for d in range(1, n):
        to = lax.rem(me + d, n)
        copies.append(remote(coarse_ref, panel.at[me], csend.at[d], crecv.at[d], {"pix": to}))
    part = wm_ref.shape[0]
    wcopies = [
        remote(wm_ref, wm.at[lat], ssem.at[2], rsem.at[2], {"lat": other}),
        remote(wn_ref, wn.at[lat], ssem.at[3], rsem.at[3], {"lat": other}),
        remote(wa_ref, wa.at[lat], ssem.at[4], rsem.at[4], {"lat": other}),
    ]
    for c in copies + wcopies:
        c.start()
    panel[me] = coarse_ref[...]
    wm[lat] = wm_ref[...]
    wn[lat] = wn_ref[...]
    wa[lat] = wa_ref[...]
    rows = lat_ref.shape[0]
    hrows = lent_ref.shape[0]
    src_ref[0:rows, :] = dot(lat_ref[...], ws_ref[...]).astype(bf16)
    rcv_ref[...] = dot(lat_ref[...], wr_ref[...]).astype(bf16)
    for c in copies:
        c.wait()
    for k in range(2):
        src_ref[rows + k * hrows : rows + (k + 1) * hrows, :] = dot(halo[k], ws_ref[...]).astype(bf16)
    base = rows + 2 * hrows
    prows = panel.shape[0] * panel.shape[1]
    flat = panel[...].astype(f32).reshape(prows, panel.shape[2]).astype(bf16)
    src_ref[base : base + prows, :] = dot(flat, ws_ref[...]).astype(bf16)
    for c in wcopies:
        c.wait()
    for k in range(2):
        wm_out[k * part : (k + 1) * part, :] = wm[k]
        wn_out[k * part : (k + 1) * part, :] = wn[k]
        wa_out[:, k * part : (k + 1) * part] = wa[k]


def one_hots(cols, t):
    lane = lax.broadcasted_iota(jnp.int32, (t, t), 1)
    return lane == cols


def edge_forward(st, rt, cols_ref, ends_ref, mask_ref, src_ref, rcv_ref, bias_ref, sum_ref, slope_ref):
    blocks, _, t = ends_ref.shape
    sum_ref[...] = jnp.zeros_like(sum_ref)
    lane = lax.broadcasted_iota(jnp.int32, (t, t), 1)
    sub = lax.broadcasted_iota(jnp.int32, (t, t), 0)
    bias = bias_ref[...]

    @pl.loop(0, blocks, unroll=4)
    def _(b):
        cols = cols_ref[b]
        oh = jnp.concatenate(
            [(cols[:, 0:1] == lane).astype(bf16), (cols[:, 1:2] == lane).astype(bf16)], axis=1
        )
        s0 = pl.multiple_of(st[b] * t, t)
        r0 = pl.multiple_of(rt[b] * t, t)
        both = jnp.concatenate([src_ref[pl.ds(s0, t), :], rcv_ref[pl.ds(r0, t), :]], axis=0)
        pre = dot(oh, both) + bias
        sig = sigmoid(pre)
        act = (pre * sig).astype(bf16)
        slope_ref[b] = (sig * (1.0 + pre * (1.0 - sig))).astype(bf16)
        ends = ends_ref[b]
        mask = mask_ref[pl.ds(b, 1), :]
        scat = ((ends[1:2, :] == sub) & (mask > 0)).astype(bf16)
        sum_ref[pl.ds(r0, t), :] += dot(scat, act)


def edge_backward(st, rt, cols_ref, ends_ref, g_ref, slope_ref, src_ref, dst_ref):
    blocks, _, t = ends_ref.shape
    src_ref[...] = jnp.zeros_like(src_ref)
    dst_ref[...] = jnp.zeros_like(dst_ref)
    lane = lax.broadcasted_iota(jnp.int32, (t, t), 1)
    sub = lax.broadcasted_iota(jnp.int32, (t, t), 0)

    @pl.loop(0, blocks, unroll=4)
    def _(b):
        cols = cols_ref[b]
        s0 = pl.multiple_of(st[b] * t, t)
        r0 = pl.multiple_of(rt[b] * t, t)
        oh = ((cols[:, 1:2] == lane) & (cols[:, 2:3] > 0)).astype(bf16)
        cot = dot(oh, g_ref[pl.ds(r0, t), :])
        pc = (cot * slope_ref[b].astype(f32)).astype(bf16)
        ends = ends_ref[b]
        src_ref[pl.ds(s0, t), :] += dot((ends[0:1, :] == sub).astype(bf16), pc)
        dst_ref[pl.ds(r0, t), :] += dot((ends[1:2, :] == sub).astype(bf16), pc)


def node_kernel(
    lat_ref, s_ref, wm_ref, wmf_ref, wself_ref, wagg_ref, waggf_ref, bias_ref, wn_ref, wnf_ref,
    gain_ref, cot_ref,
    new_ref, g_ref, grads_ref, lpart_ref, stat_ref,
    sfull, afull, nfull, ssem, rsem,
):
    lat = lax.axis_index("lat")
    other = {"lat": 1 - lat}
    part = s_ref.shape[1]

    def swap(buf, k):
        return remote(buf.at[lat], buf.at[lat], ssem.at[k], rsem.at[k], other)

    def both(buf):
        return jnp.concatenate([buf[0], buf[1]], axis=1)

    enter(1, True)
    sb = s_ref[...].astype(bf16)
    sfull[lat] = sb
    c = swap(sfull, 0)
    c.start()
    latents = lat_ref[...]
    nself = dot(latents, wself_ref[...]) + bias_ref[...]
    c.wait()
    agg = dot(both(sfull), wmf_ref[...]).astype(bf16)
    node_pre = nself + dot(agg, wagg_ref[...])
    sig = sigmoid(node_pre)
    act = (node_pre * sig).astype(bf16)
    afull[lat] = act
    c = swap(afull, 1)
    c.start()
    slope = sig * (1.0 + node_pre * (1.0 - sig))
    c.wait()
    node_out = dot(both(afull), wnf_ref[...])
    mean = jnp.mean(node_out, axis=-1, keepdims=True)
    cen = node_out - mean
    var = jnp.mean(cen * cen, axis=-1, keepdims=True)
    inv = lax.rsqrt(var + norm_eps)
    normed = cen * inv
    gain = gain_ref[...]
    new_ref[...] = (latents.astype(f32) + normed * gain).astype(bf16)
    go = cot_ref[...].astype(f32)
    dn = go * gain
    oc = inv * (
        dn
        - jnp.mean(dn, axis=-1, keepdims=True)
        - normed * jnp.mean(dn * normed, axis=-1, keepdims=True)
    )
    ocb = oc.astype(bf16)
    npc = dot_nt(ocb, wn_ref[...]) * slope
    npb = npc.astype(bf16)
    nfull[lat] = npb
    c = swap(nfull, 2)
    c.start()
    gain_sum = jnp.sum(go * normed, axis=0, keepdims=True)
    stat_ref[0:1, :] = jnp.zeros((1, part), f32)
    stat_ref[1:2, :] = jnp.sum(npc, axis=0, keepdims=True)
    stat_ref[2:3, :] = gain_sum[:, :part]
    stat_ref[3:4, :] = gain_sum[:, part:]
    stat_ref[4:8, :] = jnp.zeros((4, part), f32)
    nw = dot_tn(act, ocb).astype(bf16)
    grads_ref[0:part, :] = nw[:, :part]
    grads_ref[part : 2 * part, :] = nw[:, part:]
    width = latents.shape[1]
    grads_ref[4 * part : 4 * part + width, :] = dot_tn(latents, npb).astype(bf16)
    grads_ref[4 * part + width : 4 * part + 2 * width, :] = dot_tn(agg, npb).astype(bf16)
    lpart_ref[...] = dot_nt(npb, wself_ref[...])
    c.wait()
    ac = dot_nt(both(nfull), waggf_ref[...]).astype(bf16)
    g_ref[...] = dot_nt(ac, wm_ref[...]).astype(bf16)
    mw = dot_tn(sb, ac).astype(bf16)
    grads_ref[2 * part : 3 * part, :] = mw[:, :part]
    grads_ref[3 * part : 4 * part, :] = mw[:, part:]


def back_kernel(
    n, list_ref, ids_ref, lat_ref, src_ref, dst_ref, lpart_ref, ws_ref, wr_ref, cot_ref, stat_in,
    gl_ref, grads_ref, stat_ref,
    hs, hr, pr, own, lps, lsend, lrecv, ssem, rsem, csend, crecv,
):
    me = lax.axis_index("pix")
    lat = lax.axis_index("lat")
    right = lax.rem(me + 1, n)
    left = lax.rem(me + n - 1, n)
    rows, width = lat_ref.shape
    hrows = hs.shape[1]
    crows = pr.shape[1]
    part = src_ref.shape[1]
    base = rows + 2 * hrows
    hs[0] = src_ref[rows : rows + hrows, :].astype(bf16)
    hs[1] = src_ref[rows + hrows : base, :].astype(bf16)
    enter(n, True)
    copies = [
        remote(hs.at[0], hr.at[0], ssem.at[0], rsem.at[0], {"pix": left}),
        remote(hs.at[1], hr.at[1], ssem.at[1], rsem.at[1], {"pix": right}),
    ]
    for d in range(1, n):
        to = lax.rem(me + d, n)
        at = pl.multiple_of(base + to * crows, 8)
        copies.append(
            remote(src_ref.at[pl.ds(at, crows), :], pr.at[me], csend.at[d], crecv.at[d], {"pix": to})
        )
    for c in copies:
        c.start()
    pr[me] = src_ref[pl.ds(pl.multiple_of(base + me * crows, 8), crows), :]
    latents = lat_ref[...]
    dst = dst_ref[...]
    stat_ref[...] = stat_in[...]
    stat_ref[0:1, :] = jnp.sum(dst, axis=0, keepdims=True)
    dstb = dst.astype(bf16)
    grads_ref[width : 2 * width, :] = dot_tn(latents, dstb).astype(bf16)
    lp = lpart_ref[...] + dot_nt(dstb, wr_ref[...])
    for c in copies:
        c.wait()
    slots = list_ref.shape[0]
    t = hrows // slots
    back = hr[0].astype(f32) + hr[1].astype(f32)
    coarse = jnp.sum(pr[...], axis=0)
    sub = lax.broadcasted_iota(jnp.int32, (t, part), 0)
    for tile in range(rows // t):
        v = src_ref[tile * t : (tile + 1) * t, :]
        for k in range(slots):
            hit = jnp.full((t, part), list_ref[k], jnp.int32) == tile
            v = v + jnp.where(hit, back[k * t : (k + 1) * t, :], 0.0)
        for j in range(crows):
            hit = sub == (ids_ref[j] - tile * t)
            v = v + jnp.where(hit, coarse[j : j + 1, :], 0.0)
        own[tile * t : (tile + 1) * t, :] = v.astype(bf16)
    srcb = own[...]
    lp = lp + dot_nt(srcb, ws_ref[...])
    for k in range(2):
        half = lp[:, k * (width // 2) : (k + 1) * (width // 2)]
        lps[k] = half + cot_ref[:, k * (width // 2) : (k + 1) * (width // 2)].astype(f32)
        lsend[k] = half.astype(bf16)
    c = remote(lsend.at[1 - lat], lrecv, ssem.at[2], rsem.at[2], {"lat": 1 - lat})
    c.start()
    grads_ref[0:width, :] = dot_tn(latents, srcb).astype(bf16)
    c.wait()
    gl_ref[...] = lps[lat] + lrecv[...].astype(f32)


def reduce_kernel(
    n, scale, g_ref, stat_in, out_ref, stat_ref,
    r1, s2, r2, gathered, stats,
    p1s, p1r, l1s, l1r, l2s, l2r, p2s, p2r, ts, tr,
):
    me = lax.axis_index("pix")
    q = lax.rem(me, PLANE)
    z = me // PLANE
    m = n // PLANE
    enter(n, False)

    def plane(d):
        return {"pix": z * PLANE + lax.rem(q + d, PLANE)}

    def line(d):
        return {"pix": lax.rem(z + d, m) * PLANE + q}

    first, tiny = [], []
    for g in range(GROUPS):
        cs = []
        for d in range(1, PLANE):
            to = lax.rem(q + d, PLANE)
            cs.append(
                remote(g_ref.at[g, to], r1.at[g, d - 1], p1s.at[g, d - 1], p1r.at[g, d - 1], plane(d))
            )
            cs[-1].start()
        first.append(cs)
    for d in range(1, n):
        c = remote(stat_in, stats.at[me], ts.at[d], tr.at[d], {"pix": lax.rem(me + d, n)})
        c.start()
        tiny.append(c)
    stats[me] = stat_in[...]
    second = []
    for g in range(GROUPS):
        for c in first[g]:
            c.wait()
        acc = g_ref[g, q].astype(f32)
        for k in range(PLANE - 1):
            acc = acc + r1[g, k].astype(f32)
        s2[g] = acc.astype(bf16)
        cs = []
        for d in range(1, m):
            to = lax.rem(z + d, m)
            cs.append(remote(s2.at[g, to], r2.at[g, d - 1], l1s.at[g, d - 1], l1r.at[g, d - 1], line(d)))
            cs[-1].start()
        second.append(cs)
    third = []
    for g in range(GROUPS):
        for c in second[g]:
            c.wait()
        acc = s2[g, z].astype(f32)
        for k in range(m - 1):
            acc = acc + r2[g, k].astype(f32)
        gathered[g, q, z] = acc.astype(bf16)
        cs = []
        for d in range(1, m):
            ref = gathered.at[g, q, z]
            cs.append(remote(ref, ref, l2s.at[g, d - 1], l2r.at[g, d - 1], line(d)))
            cs[-1].start()
        third.append(cs)
    fourth = []
    for g in range(GROUPS):
        for c in third[g]:
            c.wait()
        cs = []
        for d in range(1, PLANE):
            ref = gathered.at[g, q]
            cs.append(remote(ref, ref, p2s.at[g, d - 1], p2r.at[g, d - 1], plane(d)))
            cs[-1].start()
        fourth.append(cs)
    for c in tiny:
        c.wait()
    stat_ref[...] = jnp.sum(stats[...], axis=0) * scale
    for g in range(GROUPS):
        for c in fourth[g]:
            c.wait()
        out_ref[g] = gathered[g].astype(f32) * scale


def shards(
    latents, w_send, w_recv, edge_bias, w_msg, w_self, w_agg, node_bias, w_node, norm_gain,
    coarse_ids, send_list, recv_tile, send_tile, edge_ends, edge_mask, cotangent,
):
    rows, width = latents.shape
    blocks, _, t = edge_ends.shape
    part = w_send.shape[1]
    n = lax.axis_size("pix")
    m = n // PLANE
    slots = send_list.shape[0]
    hrows = slots * t
    crows = coarse_ids.shape[0]
    srows = rows + 2 * hrows + n * crows
    dma = pltpu.SemaphoreType.DMA
    sds = jax.ShapeDtypeStruct
    scale = 1.0 / math.sqrt(rows * n)
    cols = jnp.stack([edge_ends[:, 0], edge_ends[:, 1], edge_mask], axis=-1)
    lent = latents.reshape(rows // t, t, width)[send_list].reshape(hrows, width)
    coarse = latents[coarse_ids]
    src, rcv, wmf, wnf, waf = comm_call(
        functools.partial(share_kernel, n),
        [
            sds((srows, part), bf16), sds((rows, part), bf16), sds((2 * part, width), bf16),
            sds((2 * part, width), bf16), sds((width, 2 * part), bf16),
        ],
        [VM] * 8,
        [
            pltpu.VMEM((2, hrows, width), bf16), pltpu.VMEM((n, crows, width), bf16),
            pltpu.VMEM((2, part, width), bf16), pltpu.VMEM((2, part, width), bf16),
            pltpu.VMEM((2, width, part), bf16), dma((5,)), dma((5,)), dma((n,)), dma((n,)),
        ],
        1,
    )(latents, lent, coarse, w_send, w_recv, w_msg, w_node, w_agg)
    params = pltpu.CompilerParams(vmem_limit_bytes=LIMIT)
    cost = pl.CostEstimate(flops=10**9, bytes_accessed=10**6, transcendentals=0)
    sums, slope = pl.pallas_call(
        edge_forward,
        out_shape=[sds((rows, part), f32), sds((blocks, t, part), bf16)],
        in_specs=[SM, SM] + [VM] * 6,
        out_specs=[VM, VM],
        compiler_params=params,
        cost_estimate=cost,
    )(send_tile, recv_tile, cols, edge_ends, edge_mask, src, rcv, edge_bias[None])
    new, g, grads1, lpart, stat1 = comm_call(
        node_kernel,
        [
            sds((rows, width), bf16), sds((rows, part), bf16), sds((4 * part + 2 * width, part), bf16),
            sds((rows, width), f32), sds((8, part), f32),
        ],
        [VM] * 12,
        [pltpu.VMEM((2, rows, part), bf16)] * 3 + [dma((3,)), dma((3,))],
        2,
    )(
        latents, sums, w_msg, wmf, w_self, w_agg, waf, node_bias[None], w_node, wnf,
        norm_gain[None], cotangent,
    )
    src_cot, dst_cot = pl.pallas_call(
        edge_backward,
        out_shape=[sds((srows, part), f32), sds((rows, part), f32)],
        in_specs=[SM, SM] + [VM] * 4,
        out_specs=[VM, VM],
        compiler_params=params,
        cost_estimate=cost,
    )(send_tile, recv_tile, cols, edge_ends, g, slope)
    gl, grads2, stat2 = comm_call(
        functools.partial(back_kernel, n),
        [sds((rows, width // 2), f32), sds((2 * width, part), bf16), sds((8, part), f32)],
        [SM, SM] + [VM] * 8,
        [
            pltpu.VMEM((2, hrows, part), bf16), pltpu.VMEM((2, hrows, part), bf16),
            pltpu.VMEM((n, crows, part), f32), pltpu.VMEM((rows, part), bf16),
            pltpu.VMEM((2, rows, width // 2), f32), pltpu.VMEM((2, rows, width // 2), bf16),
            pltpu.VMEM((rows, width // 2), bf16), dma((3,)), dma((3,)), dma((n,)), dma((n,)),
        ],
        3,
    )(send_list, coarse_ids, latents, src_cot, dst_cot, lpart, w_send, w_recv, cotangent, stat1)
    grads = jnp.concatenate([grads1, grads2], axis=0)
    per = grads.shape[0] // (GROUPS * n)
    shape = (GROUPS, PLANE, m, per, part)
    total, stat = comm_call(
        functools.partial(reduce_kernel, n, scale),
        [sds(shape, f32), sds((8, part), f32)],
        [VM, VM],
        [
            pltpu.VMEM((GROUPS, PLANE - 1, m, per, part), bf16),
            pltpu.VMEM((GROUPS, m, per, part), bf16),
            pltpu.VMEM((GROUPS, m - 1, per, part), bf16),
            pltpu.VMEM(shape, bf16),
            pltpu.VMEM((n, 8, part), f32),
            dma((GROUPS, PLANE - 1)), dma((GROUPS, PLANE - 1)),
            dma((GROUPS, m - 1)), dma((GROUPS, m - 1)),
            dma((GROUPS, m - 1)), dma((GROUPS, m - 1)),
            dma((GROUPS, PLANE - 1)), dma((GROUPS, PLANE - 1)),
            dma((n,)), dma((n,)),
        ],
        4,
    )(grads.reshape(shape), stat2)
    flat = total.reshape(grads.shape)

    def wide(at):
        return jnp.concatenate([flat[at : at + part], flat[at + part : at + 2 * part]], axis=1)

    a = 4 * part
    return (
        new,
        gl,
        flat[a + 2 * width : a + 3 * width],
        flat[a + 3 * width : a + 4 * width],
        stat[0],
        wide(2 * part),
        flat[a : a + width],
        flat[a + width : a + 2 * width],
        stat[1],
        wide(0),
        jnp.concatenate([stat[2], stat[3]]),
    )


def solution(mesh):
    return jax.shard_map(
        shards,
        mesh=mesh,
        in_specs=(
            P("pix", None), P(None, "lat"), P(None, "lat"), P("lat"), P("lat", None),
            P(None, "lat"), P(None, "lat"), P("lat"), P("lat", None), P(), P("pix"), P("pix"),
            P("pix"), P("pix"), P("pix", None, None), P("pix", None), P("pix", None),
        ),
        out_specs=(
            P("pix", None), P("pix", "lat"), P(None, "lat"), P(None, "lat"), P("lat"),
            P("lat", None), P(None, "lat"), P(None, "lat"), P("lat"), P("lat", None), P(),
        ),
        check_vma=False,
    )
```

time: 469 us -> 140 us (0.30)
  waiting for transfers between devices: 190 us -> 0 us
  Pallas kernels: 0 us -> 118 us
  blocking collectives: 89.4 us -> 0 us
  matrix products: 65.9 us -> 0 us
  local copies, waits for them, and re-layouts: 66.8 us -> 13.9 us
  other arithmetic: 25.2 us -> 5.35 us
  between operations: 15.2 us -> 1.37 us
  starting transfers between devices: 13 us -> 0 us
    psum x2 -> x0, waiting for transfers between devices: 128 us -> none  [the longest x1 113 us: shards(): lax.psum((send_w_grad, recv_w_grad, edge_bias_sum, msg_w_grad, self_w_gra...]
    pallas_call x0 -> x6, Pallas kernels: none -> 118 us  [the longest x1 54.2 us: shards(): comm_call(functools.partial(reduce_kernel, n, scale), [sds(shape, f32), s...]
    dot_general x26 -> x0, matrix products: 65.9 us -> none  [the longest x3 17.3 us: tile_sums(): jnp.einsum('tb,bnh->tnh', selector, per_block, precision=lax.Precision.HI...]
    reduce_scatter x2 -> x0, waiting for transfers between devices: 61.5 us -> none  [the longest x1 61.5 us: shards(): lax.psum_scatter(panel_part, 'pix', scatter_dimension=0, tiled=True)]
    psum x3 -> x0, blocking collectives: 51.3 us -> none  [the longest x1 38.7 us: shards(): lax.psum((send_w_grad, recv_w_grad, edge_bias_sum, msg_w_grad, self_w_gra...]
    gather x4 -> x1, local copies, waits for them, and re-layouts: 51.7 us -> 2.28 us  [shards(): coarse = latents[coarse_ids]]
    all_gather x1 -> x0, blocking collectives: 38.1 us -> none  [shards(): lax.all_gather(latents[coarse_ids], 'pix', axis=0, tiled=True)]
    ppermute x4 -> x0, starting transfers between devices: 12.6 us -> none  [from_behind(): return lax.ppermute(block, axis, route)]
  transfers between devices with their start and end apart: 8 -> 0, of which waited for: 3 -> 0; matrix products, arithmetic and copies ran while one was open for 12% -> 0% of each run, Pallas kernels for 0% -> 0%
where the time goes in v1:
time: 140 us; the launch traced here: 138 us
  Pallas kernels  118 us (84%)
  local copies, waits for them, and re-layouts  13.9 us (10%)
  other arithmetic  5.35 us (4%)
    pallas_call x1, Pallas kernels, shards(): comm_call(functools.partial(reduce_kernel, n, scale), [sds(shape, f32), s...  54.2 us
    pallas_call x1, Pallas kernels, shards(): comm_call(functools.partial(share_kernel, n), [sds((srows, part), bf16),...  18.5 us
    pallas_call x1, Pallas kernels, shards(): comm_call(functools.partial(back_kernel, n), [sds((rows, width // 2), f32...  14.4 us
    pallas_call x1, Pallas kernels, shards(): pl.pallas_call(edge_backward, out_shape=[sds((srows, part), f32), sds((ro...  11.3 us
    pallas_call x1, Pallas kernels, shards(): comm_call(node_kernel, [sds((rows, width), bf16), sds((rows, part), bf16)...  10.6 us
    pallas_call x1, Pallas kernels, shards(): pl.pallas_call(edge_forward, out_shape=[sds((rows, part), f32), sds((bloc...  8.73 us
    slice x1, local copies, waits for them, and re-layouts, shards(): flat[a + width:a + 2 * width]  2.95 us

profile of v1, /device:TPU:0, one launch (start us, length us, event | category | flops | bytes accessed | tf_op | source)
XLA Modules:
  0.0 138.5 jit_solution(8544714859016686307)
XLA Ops:
  1.3 0.7 compare_select_fusion
  2.0 2.3 %gather_fusion = bf16[8,512]{1,0:T(8,128)(2,1)} fusion(bf16[512,512]{1,0:T(8,128)(2,1)} %lat_ref.5, s32[1024]{0:T(1024)S(1)} %pad_clamp_fusion), kind=kCustom, calls=%fused_computation | custom fusion | bytes 16416 | tf_op jit(solution)/shard_map/gather | solution.py:412
  4.2 0.9 fusion.2
  5.1 0.7 pad_add_fusion
  5.8 1.6 %dynamic-slice_bitcast_fusion.lent_ref = bf16[128,512]{1,0:T(8,128)(2,1)} fusion(bf16[4,128,512]{2,1,0:T(8,128)(2,1)} %bitcast.21, s32[]{:T(128)} %bitcast.4), kind=kLoop, calls=%fused_computation.4 | loop fusion | bytes 262148 | tf_op jit(solution)/shard_map/reshape | solution.py:411
  7.4 2.0 %copy.37.cols_ref = s32[32,128,3]{2,1,0:T(8,128)} copy(s32[32,128,3]{1,0,2:T(8,128)S(1)} %pad_add_fusion) | data formatting | bytes 98304 | tf_op jit(solution)/shard_map/stack | solution.py:410
  9.4 18.5 %shard_map.248 = (bf16[896,256]{1,0:T(8,128)(2,1)}, bf16[512,256]{1,0:T(8,128)(2,1)}, bf16[512,512]{1,0:T(8,128)(2,1)}, bf16[512,512]{1,0:T(8,128)(2,1)}, bf16[512,512]{1,0:T(8,128)(2,1)}) custom-call(bf16[512,512]{1,0:T(8,128)(2,1)} %lat_ref.5, bf16[128,512]{1,0:T(8,128)(2,1)} %dynamic-slice_bitcast_fusion.lent_ref, bf16[8,512]{1,0:T(8,128)(2,1)} %gather_fusion, ...), custom_call_target="tpu_custom_call" | custom-call | flops 100000000 | bytes 1000000 | tf_op jit(solution)/shard_map/pallas_call | solution.py:413
  27.9 8.7 %shard_map.249 = (f32[512,256]{1,0:T(8,128)}, bf16[32,128,256]{2,1,0:T(8,128)(2,1)}) custom-call(s32[32]{0:T(128)} %st.3, s32[32]{0:T(128)} %rt.3, s32[32,128,3]{2,1,0:T(8,128)} %copy.37.cols_ref, s32[32,2,128]{2,1,0:T(2,128)} %ends_ref.3, s32[32,128]{1,0:T(8,128)} %mask_ref.1, bf16[896,256]{1,0:T(8,128)(2,1)} %get-tuple-element.30.src_ref, ...), custom_call_target="tpu_custom_call" | custom-call | flops 1000000000 | bytes 1000000 | tf_op jit(solution)/shard_map/pallas_call | solution.py:429
  36.7 10.6 %shard_map.250 = (bf16[512,512]{1,0:T(8,128)(2,1)}, bf16[512,256]{1,0:T(8,128)(2,1)}, bf16[2048,256]{1,0:T(8,128)(2,1)}, f32[512,512]{1,0:T(8,128)}, f32[8,256]{1,0:T(8,128)}) custom-call(bf16[512,512]{1,0:T(8,128)(2,1)} %lat_ref.5, f32[512,256]{1,0:T(8,128)} %get-tuple-element.32.s_ref, bf16[256,512]{1,0:T(8,128)(2,1)} %wm_ref.3, ...), custom_call_target="tpu_custom_call" | custom-call | flops 100000000 | bytes 1000000 | tf_op jit(solution)/shard_map/pallas_call | solution.py:437
  47.3 11.3 %shard_map.251 = (f32[896,256]{1,0:T(8,128)}, f32[512,256]{1,0:T(8,128)}) custom-call(s32[32]{0:T(128)} %st.3, s32[32]{0:T(128)} %rt.3, s32[32,128,3]{2,1,0:T(8,128)} %copy.37.cols_ref, s32[32,2,128]{2,1,0:T(2,128)} %ends_ref.3, bf16[512,256]{1,0:T(8,128)(2,1)} %get-tuple-element.37.g_ref, bf16[32,128,256]{2,1,0:T(8,128)(2,1)} %get-tuple-element.38.slope_ref), custom_call_target="tpu_custom_call" | custom-call | flops 1000000000 | bytes 1000000 | tf_op jit(solution)/shard_map/pallas_call | solution.py:450
  58.7 0.0 copy-start
  58.7 14.4 %shard_map.252 = (f32[512,256]{1,0:T(8,128)}, bf16[1024,256]{1,0:T(8,128)(2,1)}, f32[8,256]{1,0:T(8,128)}) custom-call(s32[1]{0:T(128)S(6)} %copy.43.list_ref, s32[8]{0:T(128)} %ids_ref.1, bf16[512,512]{1,0:T(8,128)(2,1)} %lat_ref.5, f32[896,256]{1,0:T(8,128)} %get-tuple-element.39.src_ref, f32[512,256]{1,0:T(8,128)} %get-tuple-element.40.dst_ref, ...), custom_call_target="tpu_custom_call" | custom-call | flops 100000000 | bytes 1000000 | tf_op jit(solution)/shard_map/pallas_call | solution.py:458
  73.1 0.0 copy-done
  73.1 2.3 %pad_maximum_fusion = bf16[3072,256]{1,0:T(8,128)(2,1)} fusion(bf16[1024,256]{1,0:T(8,128)(2,1)} %get-tuple-element.45, bf16[2048,256]{1,0:T(8,128)(2,1)S(1)} %copy-done), kind=kLoop, calls=%fused_computation.1 | loop fusion | flops 3145728 | bytes 3145728 | tf_op jit(solution)/shard_map/concatenate | solution.py:470
  75.4 54.2 %shard_map.253 = (f32[2,4,4,96,256]{4,3,2,1,0:T(8,128)}, f32[8,256]{1,0:T(8,128)}) custom-call(bf16[2,4,4,96,256]{4,3,2,1,0:T(8,128)(2,1)} %bitcast.20, f32[8,256]{1,0:T(8,128)} %get-tuple-element.46.stat_in), custom_call_target="tpu_custom_call" | custom-call | flops 100000000 | bytes 1000000 | tf_op jit(solution)/shard_map/pallas_call | solution.py:473
  129.6 1.4 %fusion.3 = (f32[1,256]{1,0:T(1,128)S(1)}, f32[1,256]{1,0:T(1,128)S(1)}, f32[1,256]{1,0:T(1,128)}, f32[1,256]{1,0:T(1,128)}) fusion(f32[8,256]{1,0:T(8,128)} %get-tuple-element.48), kind=kLoop, calls=%fused_computation.12 | loop fusion | bytes 8192 | tf_op jit(solution)/shard_map/slice | solution.py:508
  131.0 0.6 pad_maximum_fusion.3
  131.6 1.3 fusion
  132.8 0.0 copy-start.1
  132.8 0.0 copy-start.2
  132.8 2.9 %fusion.1 = (f32[512,256]{1,0:T(8,128)}, f32[512,256]{1,0:T(8,128)}, f32[512,256]{1,0:T(8,128)}, f32[512,256]{1,0:T(8,128)}) fusion(f32[3072,256]{1,0:T(8,128)} %bitcast.23), kind=kLoop, calls=%fused_computation.10 | loop fusion | bytes 4194304 | tf_op jit(solution)/shard_map/slice | solution.py:505
  135.8 1.1 pad_maximum_fusion.1
  136.9 0.0 copy-done.1
  136.9 0.8 copy.44
  137.7 0.0 copy-done.2
  137.7 0.8 copy.45
  (1 shorter events, 0.0 us)
Async XLA Ops:
  58.7 14.4 %copy-start = (bf16[2048,256]{1,0:T(8,128)(2,1)S(1)}, bf16[2048,256]{1,0:T(8,128)(2,1)}, u32[]{:S(2)}) copy-start(bf16[2048,256]{1,0:T(8,128)(2,1)} %get-tuple-element.44) | copy-start | bytes 3145732
  132.8 4.1 %copy-start.1 = (bf16[512,512]{1,0:T(8,128)(2,1)S(1)}, bf16[512,512]{1,0:T(8,128)(2,1)}, u32[]{:S(2)}) copy-start(bf16[512,512]{1,0:T(8,128)(2,1)} %get-tuple-element.87) | copy-start | bytes 1572868
  132.8 4.9 %copy-start.2 = (f32[512,256]{1,0:T(8,128)S(1)}, f32[512,256]{1,0:T(8,128)}, u32[]{:S(2)}) copy-start(f32[512,256]{1,0:T(8,128)} %get-tuple-element.88) | copy-start | bytes 1572868

commit v2 on v0

v2 whole, which is shorter than its diff:
```python
import functools
import math

import jax
import jax.numpy as jnp
from jax import lax
from jax.experimental import pallas as pl
from jax.experimental.pallas import tpu as pltpu
from jax.sharding import PartitionSpec as P

norm_eps = 1e-05
f32 = jnp.float32
bf16 = jnp.bfloat16
MESH = pl.DeviceIdType.MESH
VM = pl.BlockSpec(memory_space=pltpu.VMEM)
SM = pl.BlockSpec(memory_space=pltpu.SMEM)
PLANE = 4
GROUPS = 3
CHUNK = 4
LIMIT = 60 * 1024 * 1024


def dot(a, b):
    return jnp.dot(a, b, preferred_element_type=f32)


def dot_tn(a, b):
    return lax.dot_general(a, b, (((0,), (0,)), ((), ())), preferred_element_type=f32)


def dot_nt(a, b):
    return lax.dot_general(a, b, (((1,), (1,)), ((), ())), preferred_element_type=f32)


def sigmoid(v):
    return 0.5 * jnp.tanh(0.5 * v) + 0.5


def remote(src, dst, send, recv, where):
    return pltpu.make_async_remote_copy(
        src_ref=src, dst_ref=dst, send_sem=send, recv_sem=recv, device_id=where, device_id_type=MESH
    )


def enter(pix_count, partner):
    me = lax.axis_index("pix")
    barrier = pltpu.get_barrier_semaphore()
    total = 0
    for d in range(1, pix_count):
        to = lax.rem(me + d, pix_count)
        pl.semaphore_signal(barrier, inc=1, device_id={"pix": to}, device_id_type=MESH)
        total += 1
    if partner:
        other = 1 - lax.axis_index("lat")
        pl.semaphore_signal(barrier, inc=1, device_id={"lat": other}, device_id_type=MESH)
        total += 1
    pl.semaphore_wait(barrier, total)


def step_kernel(
    n, scale,
    list_ref, ids_ref, st, rt,
    lat_ref, ws_ref, wr_ref, ebias_ref, wm_ref, wself_ref, wagg_ref, nbias_ref, wn_ref, gain_ref,
    ends_ref, mask_ref, cot_ref,
    new_ref, gl_ref, gsend_ref, grecv_ref, gmsg_ref, gself_ref, gagg_ref, gnode_ref, stat_ref,
    lent, halo, mine, panel, wm, wn, wa, src_hi, src_lo, rcv_hi, rcv_lo,
    slope_ref, edge_buf, sums, sfull, afull, nfull, g_ref, src_cot, dst_cot,
    hs, hr, pr, own, lps, lsend, lrecv,
    grads, r1, s2, r2, gathered, stat_own, stats,
    ssem, rsem, csend, crecv, bsend, brecv, ts, tr,
    p1s, p1r, l1s, l1r, l2s, l2r, p2s, p2r,
):
    me = lax.axis_index("pix")
    lat = lax.axis_index("lat")
    other = {"lat": 1 - lat}
    right = lax.rem(me + 1, n)
    left = lax.rem(me + n - 1, n)
    q = lax.rem(me, PLANE)
    z = me // PLANE
    m = n // PLANE
    rows, width = lat_ref.shape
    part = ws_ref.shape[1]
    blocks, _, t = ends_ref.shape
    hrows = hs.shape[1]
    crows = pr.shape[1]
    slots = hrows // t
    base = rows + 2 * hrows
    prows = n * crows
    srows = base + prows
    per = grads.shape[3]

    def swap(buf, k):
        return remote(buf.at[lat], buf.at[lat], ssem.at[k], rsem.at[k], other)

    def plane(d):
        return {"pix": z * PLANE + lax.rem(q + d, PLANE)}

    def line(d):
        return {"pix": lax.rem(z + d, m) * PLANE + q}

    def both(buf):
        return jnp.concatenate([buf[0], buf[1]], axis=1)

    def put_grad(g, slot, value):
        count = value.shape[0] // (m * per)
        grads[g, slot : slot + count] = value.reshape(count, m, per, part).astype(bf16)

    def put_wide(g, slot, value):
        put_grad(g, slot, value[:, :part])
        put_grad(g, slot + 1, value[:, part:])

    def reduce_plane(g):
        cs = []
        for d in range(1, PLANE):
            to = lax.rem(q + d, PLANE)
            cs.append(
                remote(grads.at[g, to], r1.at[g, d - 1], p1s.at[g, d - 1], p1r.at[g, d - 1], plane(d))
            )
            cs[-1].start()
        return cs

    def reduce_line(g, before):
        for c in before:
            c.wait()
        acc = grads[g, q].astype(f32)
        for k in range(PLANE - 1):
            acc = acc + r1[g, k].astype(f32)
        s2[g] = acc.astype(bf16)
        cs = []
        for d in range(1, m):
            to = lax.rem(z + d, m)
            cs.append(remote(s2.at[g, to], r2.at[g, d - 1], l1s.at[g, d - 1], l1r.at[g, d - 1], line(d)))
            cs[-1].start()
        return cs

    def gather_line(g, before):
        for c in before:
            c.wait()
        acc = s2[g, z].astype(f32)
        for k in range(m - 1):
            acc = acc + r2[g, k].astype(f32)
        gathered[g, q, z] = acc.astype(bf16)
        ref = gathered.at[g, q, z]
        cs = []
        for d in range(1, m):
            cs.append(remote(ref, ref, l2s.at[g, d - 1], l2r.at[g, d - 1], line(d)))
            cs[-1].start()
        return cs

    def gather_plane(g, before):
        for c in before:
            c.wait()
        ref = gathered.at[g, q]
        cs = []
        for d in range(1, PLANE):
            cs.append(remote(ref, ref, p2s.at[g, d - 1], p2r.at[g, d - 1], plane(d)))
            cs[-1].start()
        return cs

    def taken(g, before, wide_ref, tall_ref, tall_first):
        for c in before:
            c.wait()
        full = (gathered[g].astype(f32) * scale).reshape(PLANE * m * per, part)
        if tall_first:
            wide_ref[...] = full[: 2 * part]
        else:
            wide_ref[:, :part] = full[:part]
            wide_ref[:, part:] = full[part : 2 * part]
        tall_ref[...] = full[2 * part :]

    enter(n, True)
    lrow = lax.broadcasted_iota(jnp.int32, (t, rows), 0)
    lcol = lax.broadcasted_iota(jnp.int32, (t, rows), 1)
    for k in range(slots):
        take = (lcol == lrow + list_ref[k] * t).astype(bf16)
        lent[k * t : (k + 1) * t, :] = dot(take, lat_ref[...]).astype(bf16)
    crow = lax.broadcasted_iota(jnp.int32, (crows, rows), 0)
    ccol = lax.broadcasted_iota(jnp.int32, (crows, rows), 1)
    pick = jnp.zeros((crows, rows), f32)
    for j in range(crows):
        pick = pick + jnp.where((crow == j) & (ccol == ids_ref[j]), 1.0, 0.0)
    mine[...] = dot(pick.astype(bf16), lat_ref[...]).astype(bf16)
    copies = [
        remote(lent, halo.at[0], ssem.at[0], rsem.at[0], {"pix": right}),
        remote(lent, halo.at[1], ssem.at[1], rsem.at[1], {"pix": left}),
    ]
    for d in range(1, n):
        to = lax.rem(me + d, n)
        copies.append(remote(mine, panel.at[me], csend.at[d], crecv.at[d], {"pix": to}))
    wcopies = [
        remote(wm_ref, wm.at[lat], ssem.at[2], rsem.at[2], other),
        remote(wn_ref, wn.at[lat], ssem.at[3], rsem.at[3], other),
        remote(wagg_ref, wa.at[lat], ssem.at[4], rsem.at[4], other),
    ]
    for c in copies + wcopies:
        c.start()
    panel[me] = mine[...]
    wm[lat] = wm_ref[...]
    wn[lat] = wn_ref[...]
    wa[lat] = wagg_ref[...]

    def split(hi, lo, at, value):
        top = value.astype(bf16)
        rest = (value - top.astype(f32)).astype(bf16)
        for k in range(value.shape[0] // t):
            hi[at // t + k] = top[k * t : (k + 1) * t, :]
            lo[at // t + k] = rest[k * t : (k + 1) * t, :]

    split(src_hi, src_lo, 0, dot(lat_ref[...], ws_ref[...]))
    split(rcv_hi, rcv_lo, 0, dot(lat_ref[...], wr_ref[...]))
    nself = dot(lat_ref[...], wself_ref[...]) + nbias_ref[...]
    for c in copies:
        c.wait()
    for k in range(2):
        split(src_hi, src_lo, rows + k * hrows, dot(halo[k], ws_ref[...]))
    flat = panel[...].astype(f32).reshape(prows, width).astype(bf16)
    split(src_hi, src_lo, base, dot(flat, ws_ref[...]))

    sub = lax.broadcasted_iota(jnp.int32, (t, t), 0)
    ebias = ebias_ref[...]

    @pl.loop(0, blocks, unroll=4)
    def _(b):
        ends = ends_ref[b]
        oh_s = (ends[0:1, :] == sub).astype(bf16)
        oh_r = (ends[1:2, :] == sub).astype(bf16)
        oh = jnp.concatenate([oh_s, oh_r, oh_s, oh_r], axis=0)
        s0 = st[b]
        r0 = rt[b]
        tabs = jnp.concatenate([src_hi[s0], rcv_hi[r0], src_lo[s0], rcv_lo[r0]], axis=0)
        pre = dot_tn(oh, tabs) + ebias
        sig = sigmoid(pre)
        edge_buf[b] = (pre * sig).astype(bf16)
        slope_ref[b] = sig * (1.0 + pre * (1.0 - sig))

    def ids_row(c, end, tile_ref):
        parts = []
        for i in range(CHUNK):
            b = c * CHUNK + i
            parts.append(ends_ref[b][end : end + 1, :] + tile_ref[b] * t)
        return jnp.concatenate(parts, axis=1)

    def edge_rows(c):
        return jnp.concatenate([edge_buf[c * CHUNK + i] for i in range(CHUNK)], axis=0)

    wide_sub = lax.broadcasted_iota(jnp.int32, (rows, CHUNK * t), 0)
    src_sub = lax.broadcasted_iota(jnp.int32, (srows, CHUNK * t), 0)
    sums[...] = jnp.zeros_like(sums)

    @pl.loop(0, blocks // CHUNK)
    def _(c):
        live = jnp.concatenate([mask_ref[pl.ds(c * CHUNK + i, 1), :] for i in range(CHUNK)], axis=1)
        goal = jnp.where(live > 0, ids_row(c, 1, rt), -1)
        sums[...] += dot((wide_sub == goal).astype(bf16), edge_rows(c))

    sb = sums[...].astype(bf16)
    sfull[lat] = sb
    cs = swap(sfull, 5)
    cs.start()
    for c in wcopies:
        c.wait()
    wmf = jnp.concatenate([wm[0], wm[1]], axis=0)
    cs.wait()
    agg = dot(both(sfull), wmf).astype(bf16)
    node_pre = nself + dot(agg, wagg_ref[...])
    sig = sigmoid(node_pre)
    act = (node_pre * sig).astype(bf16)
    afull[lat] = act
    cs = swap(afull, 6)
    cs.start()
    slope = sig * (1.0 + node_pre * (1.0 - sig))
    wnf = jnp.concatenate([wn[0], wn[1]], axis=0)
    cs.wait()
    node_out = dot(both(afull), wnf)
    mean = jnp.mean(node_out, axis=-1, keepdims=True)
    cen = node_out - mean
    var = jnp.mean(cen * cen, axis=-1, keepdims=True)
    inv = lax.rsqrt(var + norm_eps)
    normed = cen * inv
    gain = gain_ref[...]
    new_ref[...] = (lat_ref[...].astype(f32) + normed * gain).astype(bf16)
    go = cot_ref[...].astype(f32)
    dn = go * gain
    oc = inv * (
        dn
        - jnp.mean(dn, axis=-1, keepdims=True)
        - normed * jnp.mean(dn * normed, axis=-1, keepdims=True)
    )
    ocb = oc.astype(bf16)
    npc = dot_nt(ocb, wn_ref[...]) * slope
    npb = npc.astype(bf16)
    nfull[lat] = npb
    cs = swap(nfull, 7)
    cs.start()
    put_wide(0, 0, dot_tn(act, ocb))
    put_grad(0, 2, dot_tn(lat_ref[...], npb))
    a0 = reduce_plane(0)
    gain_sum = jnp.sum(go * normed, axis=0, keepdims=True)
    stat_own[1:2, :] = jnp.sum(npc, axis=0, keepdims=True)
    stat_own[2:3, :] = gain_sum[:, :part]
    stat_own[3:4, :] = gain_sum[:, part:]
    stat_own[4:8, :] = jnp.zeros((4, part), f32)
    cs.wait()
    ac = dot_nt(both(nfull), both(wa)).astype(bf16)
    back_part = dot_nt(ac, wm_ref[...]).astype(bf16)
    for k in range(rows // t):
        g_ref[k] = back_part[k * t : (k + 1) * t, :]
    put_wide(1, 0, dot_tn(sb, ac))
    put_grad(1, 2, dot_tn(agg, npb))
    a1 = reduce_plane(1)

    @pl.loop(0, blocks, unroll=4)
    def _(b):
        ends = ends_ref[b]
        r0 = rt[b]
        oh = ((ends[1:2, :] == sub) & (mask_ref[pl.ds(b, 1), :] > 0)).astype(bf16)
        edge_buf[b] = (dot_tn(oh, g_ref[r0]) * slope_ref[b]).astype(bf16)

    src_cot[...] = jnp.zeros_like(src_cot)

    @pl.loop(0, blocks // CHUNK)
    def _(c):
        src_cot[...] += dot((src_sub == ids_row(c, 0, st)).astype(bf16), edge_rows(c))

    hs[0] = src_cot[rows : rows + hrows, :].astype(bf16)
    hs[1] = src_cot[rows + hrows : base, :].astype(bf16)
    copies = [
        remote(hs.at[0], hr.at[0], ssem.at[8], rsem.at[8], {"pix": left}),
        remote(hs.at[1], hr.at[1], ssem.at[9], rsem.at[9], {"pix": right}),
    ]
    for d in range(1, n):
        to = lax.rem(me + d, n)
        at = pl.multiple_of(base + to * crows, 8)
        copies.append(
            remote(src_cot.at[pl.ds(at, crows), :], pr.at[me], bsend.at[d], brecv.at[d], {"pix": to})
        )
    for c in copies:
        c.start()
    pr[me] = src_cot[pl.ds(pl.multiple_of(base + me * crows, 8), crows), :]
    a0 = reduce_line(0, a0)
    dst_cot[...] = jnp.zeros_like(dst_cot)

    @pl.loop(0, blocks // CHUNK)
    def _(c):
        dst_cot[...] += dot((wide_sub == ids_row(c, 1, rt)).astype(bf16), edge_rows(c))

    dst = dst_cot[...]
    stat_own[0:1, :] = jnp.sum(dst, axis=0, keepdims=True)
    tiny = []
    for d in range(1, n):
        c = remote(stat_own, stats.at[me], ts.at[d], tr.at[d], {"pix": lax.rem(me + d, n)})
        c.start()
        tiny.append(c)
    stats[me] = stat_own[...]
    dstb = dst.astype(bf16)
    a1 = reduce_line(1, a1)
    a0 = gather_line(0, a0)
    for c in copies:
        c.wait()
    back = hr[0].astype(f32) + hr[1].astype(f32)
    coarse = jnp.sum(pr[...], axis=0)
    tsub = lax.broadcasted_iota(jnp.int32, (t, part), 0)
    for tile in range(rows // t):
        v = src_cot[tile * t : (tile + 1) * t, :]
        for k in range(slots):
            hit = jnp.full((t, part), list_ref[k], jnp.int32) == tile
            v = v + jnp.where(hit, back[k * t : (k + 1) * t, :], 0.0)
        for j in range(crows):
            v = v + jnp.where(tsub == (ids_ref[j] - tile * t), coarse[j : j + 1, :], 0.0)
        own[tile * t : (tile + 1) * t, :] = v.astype(bf16)
    srcb = own[...]
    put_grad(2, 0, dot_tn(lat_ref[...], srcb))
    put_grad(2, 2, dot_tn(lat_ref[...], dstb))
    a2 = reduce_plane(2)
    lp = dot_nt(npb, wself_ref[...]) + dot_nt(dstb, wr_ref[...]) + dot_nt(srcb, ws_ref[...])
    half = width // 2
    for k in range(2):
        piece = lp[:, k * half : (k + 1) * half]
        lps[k] = piece + cot_ref[:, k * half : (k + 1) * half].astype(f32)
        lsend[k] = piece.astype(bf16)
    cs = remote(lsend.at[1 - lat], lrecv, ssem.at[10], rsem.at[10], other)
    cs.start()
    a0 = gather_plane(0, a0)
    a1 = gather_line(1, a1)
    cs.wait()
    gl_ref[...] = lps[lat] + lrecv[...].astype(f32)
    a1 = gather_plane(1, a1)
    a2 = reduce_line(2, a2)
    for c in tiny:
        c.wait()
    stat_ref[...] = jnp.sum(stats[...], axis=0) * scale
    a2 = gather_line(2, a2)
    taken(0, a0, gnode_ref, gself_ref, False)
    a2 = gather_plane(2, a2)
    taken(1, a1, gmsg_ref, gagg_ref, False)
    taken(2, a2, gsend_ref, grecv_ref, True)


def shards(
    latents, w_send, w_recv, edge_bias, w_msg, w_self, w_agg, node_bias, w_node, norm_gain,
    coarse_ids, send_list, recv_tile, send_tile, edge_ends, edge_mask, cotangent,
):
    rows, width = latents.shape
    blocks, _, t = edge_ends.shape
    part = w_send.shape[1]
    n = lax.axis_size("pix")
    m = n // PLANE
    hrows = send_list.shape[0] * t
    crows = coarse_ids.shape[0]
    srows = rows + 2 * hrows + n * crows
    per = 4 * part // n
    half = width // 2
    dma = pltpu.SemaphoreType.DMA
    sds = jax.ShapeDtypeStruct
    V = pltpu.VMEM
    scale = 1.0 / math.sqrt(rows * n)
    tall = sds((width, part), f32)
    broad = sds((part, width), f32)
    outs = [sds((rows, width), bf16), sds((rows, half), f32), tall, tall, broad, tall, tall, broad, sds((8, part), f32)]
    line_sems = [dma((GROUPS, m - 1))] * 4
    plane_sems = [dma((GROUPS, PLANE - 1))] * 2
    res = pl.pallas_call(
        functools.partial(step_kernel, n, scale),
        out_shape=outs,
        in_specs=[SM] * 4 + [VM] * 13,
        out_specs=[VM] * len(outs),
        scratch_shapes=[
            V((hrows, width), bf16), V((2, hrows, width), bf16),
            V((crows, width), bf16), V((n, crows, width), bf16),
            V((2, part, width), bf16), V((2, part, width), bf16), V((2, width, part), bf16),
            V((srows // t, t, part), bf16), V((srows // t, t, part), bf16), V((rows // t, t, part), bf16), V((rows // t, t, part), bf16),
            V((blocks, t, part), f32), V((blocks, t, part), bf16), V((rows, part), f32),
            V((2, rows, part), bf16), V((2, rows, part), bf16), V((2, rows, part), bf16),
            V((rows // t, t, part), bf16), V((srows, part), f32), V((rows, part), f32),
            V((2, hrows, part), bf16), V((2, hrows, part), bf16), V((n, crows, part), f32),
            V((rows, part), bf16), V((2, rows, half), f32), V((2, rows, half), bf16), V((rows, half), bf16),
            V((GROUPS, PLANE, m, per, part), bf16), V((GROUPS, PLANE - 1, m, per, part), bf16),
            V((GROUPS, m, per, part), bf16), V((GROUPS, m - 1, per, part), bf16),
            V((GROUPS, PLANE, m, per, part), bf16), V((8, part), f32), V((n, 8, part), f32),
            dma((11,)), dma((11,)), dma((n,)), dma((n,)), dma((n,)), dma((n,)), dma((n,)), dma((n,)),
        ] + plane_sems + line_sems + plane_sems,
        compiler_params=pltpu.CompilerParams(
            collective_id=1, has_side_effects=True, vmem_limit_bytes=LIMIT
        ),
    )(
        send_list, coarse_ids, send_tile, recv_tile, latents, w_send, w_recv, edge_bias[None], w_msg,
        w_self, w_agg, node_bias[None], w_node, norm_gain[None], edge_ends, edge_mask, cotangent,
    )
    new, gl, gsend, grecv, gmsg, gself, gagg, gnode, stat = res
    return (
        new, gl, gsend, grecv, stat[0], gmsg, gself, gagg, stat[1], gnode,
        jnp.concatenate([stat[2], stat[3]]),
    )


def solution(mesh):
    return jax.shard_map(
        shards,
        mesh=mesh,
        in_specs=(
            P("pix", None), P(None, "lat"), P(None, "lat"), P("lat"), P("lat", None),
            P(None, "lat"), P(None, "lat"), P("lat"), P("lat", None), P(), P("pix"), P("pix"),
            P("pix"), P("pix"), P("pix", None, None), P("pix", None), P("pix", None),
        ),
        out_specs=(
            P("pix", None), P("pix", "lat"), P(None, "lat"), P(None, "lat"), P("lat"),
            P("lat", None), P(None, "lat"), P(None, "lat"), P("lat"), P("lat", None), P(),
        ),
        check_vma=False,
    )
```

time: 469 us -> 90.5 us (0.19)
  waiting for transfers between devices: 190 us -> 0 us
  blocking collectives: 89.4 us -> 0 us
  Pallas kernels: 0 us -> 76.5 us
  matrix products: 65.9 us -> 0 us
  local copies, waits for them, and re-layouts: 66.8 us -> 11.5 us
  other arithmetic: 25.2 us -> 0.58 us
  between operations: 15.2 us -> 1.32 us
  starting transfers between devices: 13 us -> 0 us
    psum x2 -> x0, waiting for transfers between devices: 128 us -> none  [the longest x1 113 us: shards(): lax.psum((send_w_grad, recv_w_grad, edge_bias_sum, msg_w_grad, self_w_gra...]
    pallas_call x0 -> x1, Pallas kernels: none -> 76.5 us  [shards(): pl.pallas_call(functools.partial(step_kernel, n, scale), out_shape=outs,...]
    dot_general x26 -> x0, matrix products: 65.9 us -> none  [the longest x3 17.3 us: tile_sums(): jnp.einsum('tb,bnh->tnh', selector, per_block, precision=lax.Precision.HI...]
    reduce_scatter x2 -> x0, waiting for transfers between devices: 61.5 us -> none  [the longest x1 61.5 us: shards(): lax.psum_scatter(panel_part, 'pix', scatter_dimension=0, tiled=True)]
    gather x4 -> x0, local copies, waits for them, and re-layouts: 51.7 us -> none  [the longest x2 32.3 us: shards(): edge_pre = source_proj[senders] + recv_proj[receivers] + edge_bias]
    psum x3 -> x0, blocking collectives: 51.3 us -> none  [the longest x1 38.7 us: shards(): lax.psum((send_w_grad, recv_w_grad, edge_bias_sum, msg_w_grad, self_w_gra...]
    all_gather x1 -> x0, blocking collectives: 38.1 us -> none  [shards(): lax.all_gather(latents[coarse_ids], 'pix', axis=0, tiled=True)]
    ppermute x4 -> x0, starting transfers between devices: 12.6 us -> none  [from_behind(): return lax.ppermute(block, axis, route)]
  transfers between devices with their start and end apart: 8 -> 0, of which waited for: 3 -> 0; matrix products, arithmetic and copies ran while one was open for 12% -> 0% of each run, Pallas kernels for 0% -> 0%
where the time goes in v2:
time: 90.5 us; the launch traced here: 89.9 us
  Pallas kernels  76.5 us (85%)
  local copies, waits for them, and re-layouts  11.5 us (13%)
  between operations  1.32 us (1%)
    pallas_call x1, Pallas kernels, shards(): pl.pallas_call(functools.partial(step_kernel, n, scale), out_shape=outs,...  76.5 us
    unnamed x22, local copies, waits for them, and re-layouts  10.1 us

profile of v2, /device:TPU:0, one launch (start us, length us, event | category | flops | bytes accessed | tf_op | source)
XLA Modules:
  0.0 89.9 jit_solution(7203800719708266231)
XLA Ops:
  1.3 76.5 %shard_map.248 = (bf16[512,512]{1,0:T(8,128)(2,1)}, f32[512,256]{1,0:T(8,128)}, f32[512,256]{1,0:T(8,128)}, f32[512,256]{1,0:T(8,128)}, f32[256,512]{1,0:T(8,128...) custom-call(s32[1]{0:T(128)S(6)} %copy.36.list_ref, s32[8]{0:T(128)} %ids_ref.1, ...), custom_call_target="tpu_custom_call" | custom-call | tf_op jit(solution)/shard_map/pallas_call | solution.py:422
  77.8 1.4 %fusion = (f32[1,256]{1,0:T(1,128)S(1)}, f32[1,256]{1,0:T(1,128)S(1)}, f32[1,256]{1,0:T(1,128)}, f32[1,256]{1,0:T(1,128)}) fusion(f32[8,256]{1,0:T(8,128)} %get-tuple-element.24), kind=kLoop, calls=%fused_computation.1 | loop fusion | bytes 8192 | tf_op jit(solution)/shard_map/slice | solution.py:452
  79.2 0.6 pad_maximum_fusion
  79.8 0.0 copy-start.6
  79.8 1.9 %copy.37 = bf16[512,512]{1,0:T(8,128)(2,1)} copy(bf16[512,512]{1,0:T(8,128)(2,1)} %get-tuple-element.44) | data formatting | bytes 1048576
  81.7 0.0 copy-done.6
  81.7 0.0 copy-start.5
  81.7 0.8 copy.38
  82.5 0.4 copy-done.5
  82.9 0.0 copy-start.4
  82.9 0.8 copy.39
  83.7 0.4 copy-done.4
  84.2 0.0 copy-start.3
  84.2 0.8 copy.40
  85.0 0.4 copy-done.3
  85.4 0.0 copy-start.2
  85.4 0.8 copy.41
  86.2 0.4 copy-done.2
  86.6 0.0 copy-start.1
  86.6 0.8 copy.42
  87.4 0.4 copy-done.1
  87.9 0.0 copy-start
  87.9 0.8 copy.43
  88.7 0.4 copy-done
  89.1 0.8 copy.44
Async XLA Ops:
  79.8 1.9 %copy-start.6 = (f32[512,256]{1,0:T(8,128)S(1)}, f32[512,256]{1,0:T(8,128)}, u32[]{:S(2)}) copy-start(f32[512,256]{1,0:T(8,128)} %get-tuple-element.45) | copy-start | bytes 1572868
  81.7 1.2 %copy-start.5 = (f32[512,256]{1,0:T(8,128)S(1)}, f32[512,256]{1,0:T(8,128)}, u32[]{:S(2)}) copy-start(f32[512,256]{1,0:T(8,128)} %get-tuple-element.46) | copy-start | bytes 1572868
  82.9 1.2 %copy-start.4 = (f32[512,256]{1,0:T(8,128)S(1)}, f32[512,256]{1,0:T(8,128)}, u32[]{:S(2)}) copy-start(f32[512,256]{1,0:T(8,128)} %get-tuple-element.47) | copy-start | bytes 1572868
  84.2 1.2 %copy-start.3 = (f32[256,512]{1,0:T(8,128)S(1)}, f32[256,512]{1,0:T(8,128)}, u32[]{:S(2)}) copy-start(f32[256,512]{1,0:T(8,128)} %get-tuple-element.49) | copy-start | bytes 1572868
  85.4 1.2 %copy-start.2 = (f32[512,256]{1,0:T(8,128)S(1)}, f32[512,256]{1,0:T(8,128)}, u32[]{:S(2)}) copy-start(f32[512,256]{1,0:T(8,128)} %get-tuple-element.50) | copy-start | bytes 1572868
  86.6 1.2 %copy-start.1 = (f32[512,256]{1,0:T(8,128)S(1)}, f32[512,256]{1,0:T(8,128)}, u32[]{:S(2)}) copy-start(f32[512,256]{1,0:T(8,128)} %get-tuple-element.51) | copy-start | bytes 1572868
  87.9 1.2 %copy-start = (f32[256,512]{1,0:T(8,128)S(1)}, f32[256,512]{1,0:T(8,128)}, u32[]{:S(2)}) copy-start(f32[256,512]{1,0:T(8,128)} %get-tuple-element.53) | copy-start | bytes 1572868

commit v3 on v2

--- a/solution.py
+++ b/solution.py
@@ -66,7 +66,7 @@
     lent, halo, mine, panel, wm, wn, wa, src_hi, src_lo, rcv_hi, rcv_lo,
     slope_ref, edge_buf, sums, sfull, afull, nfull, g_ref, src_cot, dst_cot,
     hs, hr, pr, own, lps, lsend, lrecv,
-    grads, r1, s2, r2, gathered, stat_own, stats,
+    grads, r1, s2, r2, gathered, stat_own, stats, lat_t,
     ssem, rsem, csend, crecv, bsend, brecv, ts, tr,
     p1s, p1r, l1s, l1r, l2s, l2r, p2s, p2r,
 ):
@@ -209,6 +209,7 @@
     split(src_hi, src_lo, 0, dot(lat_ref[...], ws_ref[...]))
     split(rcv_hi, rcv_lo, 0, dot(lat_ref[...], wr_ref[...]))
     nself = dot(lat_ref[...], wself_ref[...]) + nbias_ref[...]
+    lat_t[...] = lat_ref[...].T
     for c in copies:
         c.wait()
     for k in range(2):
@@ -216,19 +217,20 @@
     flat = panel[...].astype(f32).reshape(prows, width).astype(bf16)
     split(src_hi, src_lo, base, dot(flat, ws_ref[...]))
 
-    sub = lax.broadcasted_iota(jnp.int32, (t, t), 0)
+    lane = lax.broadcasted_iota(jnp.int32, (t, t), 1)
     ebias = ebias_ref[...]
 
     @pl.loop(0, blocks, unroll=4)
     def _(b):
         ends = ends_ref[b]
-        oh_s = (ends[0:1, :] == sub).astype(bf16)
-        oh_r = (ends[1:2, :] == sub).astype(bf16)
-        oh = jnp.concatenate([oh_s, oh_r, oh_s, oh_r], axis=0)
+        cols = jnp.concatenate([ends] * 4, axis=0).T
+        oh_s = (cols[:, 0:1] == lane).astype(bf16)
+        oh_r = (cols[:, 1:2] == lane).astype(bf16)
+        oh = jnp.concatenate([oh_s, oh_r, oh_s, oh_r], axis=1)
         s0 = st[b]
         r0 = rt[b]
         tabs = jnp.concatenate([src_hi[s0], rcv_hi[r0], src_lo[s0], rcv_lo[r0]], axis=0)
-        pre = dot_tn(oh, tabs) + ebias
+        pre = dot(oh, tabs) + ebias
         sig = sigmoid(pre)
         edge_buf[b] = (pre * sig).astype(bf16)
         slope_ref[b] = sig * (1.0 + pre * (1.0 - sig))
@@ -293,7 +295,7 @@
     cs = swap(nfull, 7)
     cs.start()
     put_wide(0, 0, dot_tn(act, ocb))
-    put_grad(0, 2, dot_tn(lat_ref[...], npb))
+    put_grad(0, 2, dot(lat_t[...], npb))
     a0 = reduce_plane(0)
     gain_sum = jnp.sum(go * normed, axis=0, keepdims=True)
     stat_own[1:2, :] = jnp.sum(npc, axis=0, keepdims=True)
@@ -313,8 +315,10 @@
     def _(b):
         ends = ends_ref[b]
         r0 = rt[b]
-        oh = ((ends[1:2, :] == sub) & (mask_ref[pl.ds(b, 1), :] > 0)).astype(bf16)
-        edge_buf[b] = (dot_tn(oh, g_ref[r0]) * slope_ref[b]).astype(bf16)
+        goal = jnp.where(mask_ref[pl.ds(b, 1), :] > 0, ends[1:2, :], -1)
+        cols = jnp.concatenate([goal] * 8, axis=0).T
+        oh = (cols[:, 0:1] == lane).astype(bf16)
+        edge_buf[b] = (dot(oh, g_ref[r0]) * slope_ref[b]).astype(bf16)
 
     src_cot[...] = jnp.zeros_like(src_cot)
 
@@ -353,6 +357,8 @@
         tiny.append(c)
     stats[me] = stat_own[...]
     dstb = dst.astype(bf16)
+    put_grad(2, 2, dot(lat_t[...], dstb))
+    lp = dot_nt(npb, wself_ref[...]) + dot_nt(dstb, wr_ref[...])
     a1 = reduce_line(1, a1)
     a0 = gather_line(0, a0)
     for c in copies:
@@ -369,10 +375,9 @@
             v = v + jnp.where(tsub == (ids_ref[j] - tile * t), coarse[j : j + 1, :], 0.0)
         own[tile * t : (tile + 1) * t, :] = v.astype(bf16)
     srcb = own[...]
-    put_grad(2, 0, dot_tn(lat_ref[...], srcb))
-    put_grad(2, 2, dot_tn(lat_ref[...], dstb))
+    put_grad(2, 0, dot(lat_t[...], srcb))
     a2 = reduce_plane(2)
-    lp = dot_nt(npb, wself_ref[...]) + dot_nt(dstb, wr_ref[...]) + dot_nt(srcb, ws_ref[...])
+    lp = lp + dot_nt(srcb, ws_ref[...])
     half = width // 2
     for k in range(2):
         piece = lp[:, k * half : (k + 1) * half]
@@ -436,7 +441,7 @@
             V((rows, part), bf16), V((2, rows, half), f32), V((2, rows, half), bf16), V((rows, half), bf16),
             V((GROUPS, PLANE, m, per, part), bf16), V((GROUPS, PLANE - 1, m, per, part), bf16),
             V((GROUPS, m, per, part), bf16), V((GROUPS, m - 1, per, part), bf16),
-            V((GROUPS, PLANE, m, per, part), bf16), V((8, part), f32), V((n, 8, part), f32),
+            V((GROUPS, PLANE, m, per, part), bf16), V((8, part), f32), V((n, 8, part), f32), V((width, rows), bf16),
             dma((11,)), dma((11,)), dma((n,)), dma((n,)), dma((n,)), dma((n,)), dma((n,)), dma((n,)),
         ] + plane_sems + line_sems + plane_sems,
         compiler_params=pltpu.CompilerParams(

time: 90.5 us -> 92.5 us (1.022)
  Pallas kernels: 76.5 us -> 78.5 us
    pallas_call x1, Pallas kernels: 76.5 us -> 78.5 us  [shards(): pl.pallas_call(functools.partial(step_kernel, n, scale), out_shape=outs,...]
where the time goes in v3:
time: 92.5 us; the launch traced here: 91.9 us
  Pallas kernels  78.5 us (85%)
  local copies, waits for them, and re-layouts  11.5 us (12%)
  between operations  1.32 us (1%)
    pallas_call x1, Pallas kernels, shards(): pl.pallas_call(functools.partial(step_kernel, n, scale), out_shape=outs,...  78.5 us
    unnamed x22, local copies, waits for them, and re-layouts  10.1 us

profile of v3, /device:TPU:0, one launch (start us, length us, event | category | flops | bytes accessed | tf_op | source)
XLA Modules:
  0.0 91.9 jit_solution(3280194479218175509)
XLA Ops:
  1.3 78.5 %shard_map.248 = (bf16[512,512]{1,0:T(8,128)(2,1)}, f32[512,256]{1,0:T(8,128)}, f32[512,256]{1,0:T(8,128)}, f32[512,256]{1,0:T(8,128)}, f32[256,512]{1,0:T(8,128...) custom-call(s32[1]{0:T(128)S(6)} %copy.36.list_ref, s32[8]{0:T(128)} %ids_ref.1, ...), custom_call_target="tpu_custom_call" | custom-call | tf_op jit(solution)/shard_map/pallas_call | solution.py:427
  79.8 1.4 %fusion = (f32[1,256]{1,0:T(1,128)S(1)}, f32[1,256]{1,0:T(1,128)S(1)}, f32[1,256]{1,0:T(1,128)}, f32[1,256]{1,0:T(1,128)}) fusion(f32[8,256]{1,0:T(8,128)} %get-tuple-element.24), kind=kLoop, calls=%fused_computation.1 | loop fusion | bytes 8192 | tf_op jit(solution)/shard_map/slice | solution.py:457
  81.2 0.6 pad_maximum_fusion
  81.8 0.0 copy-start.6
  81.8 1.9 %copy.37 = bf16[512,512]{1,0:T(8,128)(2,1)} copy(bf16[512,512]{1,0:T(8,128)(2,1)} %get-tuple-element.44) | data formatting | bytes 1048576
  83.7 0.0 copy-done.6
  83.7 0.0 copy-start.5
  83.7 0.8 copy.38
  84.5 0.4 copy-done.5
  84.9 0.0 copy-start.4
  84.9 0.8 copy.39
  85.7 0.4 copy-done.4
  86.2 0.0 copy-start.3
  86.2 0.8 copy.40
  87.0 0.4 copy-done.3
  87.4 0.0 copy-start.2
  87.4 0.8 copy.41
  88.2 0.4 copy-done.2
  88.6 0.0 copy-start.1
  88.6 0.8 copy.42
  89.4 0.4 copy-done.1
  89.9 0.0 copy-start
  89.9 0.8 copy.43
  90.7 0.4 copy-done
  91.1 0.8 copy.44
Async XLA Ops:
  81.8 1.9 %copy-start.6 = (f32[512,256]{1,0:T(8,128)S(1)}, f32[512,256]{1,0:T(8,128)}, u32[]{:S(2)}) copy-start(f32[512,256]{1,0:T(8,128)} %get-tuple-element.45) | copy-start | bytes 1572868
  83.7 1.2 %copy-start.5 = (f32[512,256]{1,0:T(8,128)S(1)}, f32[512,256]{1,0:T(8,128)}, u32[]{:S(2)}) copy-start(f32[512,256]{1,0:T(8,128)} %get-tuple-element.46) | copy-start | bytes 1572868
  84.9 1.2 %copy-start.4 = (f32[512,256]{1,0:T(8,128)S(1)}, f32[512,256]{1,0:T(8,128)}, u32[]{:S(2)}) copy-start(f32[512,256]{1,0:T(8,128)} %get-tuple-element.47) | copy-start | bytes 1572868
  86.2 1.2 %copy-start.3 = (f32[256,512]{1,0:T(8,128)S(1)}, f32[256,512]{1,0:T(8,128)}, u32[]{:S(2)}) copy-start(f32[256,512]{1,0:T(8,128)} %get-tuple-element.49) | copy-start | bytes 1572868
  87.4 1.2 %copy-start.2 = (f32[512,256]{1,0:T(8,128)S(1)}, f32[512,256]{1,0:T(8,128)}, u32[]{:S(2)}) copy-start(f32[512,256]{1,0:T(8,128)} %get-tuple-element.50) | copy-start | bytes 1572868
  88.6 1.2 %copy-start.1 = (f32[512,256]{1,0:T(8,128)S(1)}, f32[512,256]{1,0:T(8,128)}, u32[]{:S(2)}) copy-start(f32[512,256]{1,0:T(8,128)} %get-tuple-element.51) | copy-start | bytes 1572868
  89.9 1.2 %copy-start = (f32[256,512]{1,0:T(8,128)S(1)}, f32[256,512]{1,0:T(8,128)}, u32[]{:S(2)}) copy-start(f32[256,512]{1,0:T(8,128)} %get-tuple-element.53) | copy-start | bytes 1572868
